TPU v7x, 128 devices: a whole 4x4x4 slice. The times are simulated.
128 devices in a mesh: seq: 128 (over x, z, y, core).
Axes of the slice: x: 4, y: 4, z: 4, core: 2. Of those that a mesh axis runs over, the one named last changes fastest.
Arguments:
- acceptance_gate: bfloat16 [16384, 2048], P('seq'), may hold values from -1.1953125 to 1.1953125
- lookup_matrix: bfloat16 [16384, 2048], P('seq'), may hold values from -0.29882812 to 0.29882812
- payload_matrix: bfloat16 [16384, 2048], P('seq'), may hold values from -6 to 6
- fading_parameter: float32 [16384, 2048], P('seq'), may hold values from -17 to 0.5
- present_reward: float32 [2048], replicated, may hold values from -4 to 4
- emitted_cotangent: bfloat16 [16384, 2048], P('seq'), may hold values from -0.119628906 to 0.119628906
- paper_spans: int32 [256], replicated, may hold values from 1 to 4096, 16384 in all
Outputs:
- grad_receptance: bfloat16 [16384, 2048], P('seq')
- grad_key: bfloat16 [16384, 2048], P('seq')
- grad_value: bfloat16 [16384, 2048], P('seq')
- grad_decay: bfloat16 [16384, 2048], P('seq')
- reward_cotangent: float32 [2048], replicated
Inputs may be any that keep to these rules, and one draw needn't show every extreme that they name: `paper_spans`: the 256 documents fill the packed sequence of 16384 tokens in order.
All inputs are finite; a program needn't handle non-finite values.
Results may differ from a plain program's by a relative error of at most 0.001.
Values sent between devices are 32-bit elements; how exact they have to be, the bound alone decides.
No kernel may reach another device: no remote copies, remote signals or barrier semaphores. Data moves between devices by JAX's collectives and lax.ppermute only.
A program may use at most 320 MiB of HBM per device.

v0:
```python
import jax
import jax.numpy as jnp
from jax import lax
from jax.sharding import Mesh
from jax.sharding import PartitionSpec as P

HS = 64
SEQ = ("seq_0", "seq_1", "seq_2", "seq_3")


def filled_with(shard, identity):
    return jax.tree.map(
        lambda a, e: jnp.broadcast_to(jnp.asarray(e, a.dtype), a.shape), shard, identity
    )


def entering(shard, axes, combine, identity, reverse):
    before = start = filled_with(shard, identity)
    total = shard
    for axis in reversed(axes):
        size, position = (lax.axis_size(axis), lax.axis_index(axis))
        pieces = jax.tree.map(lambda part: lax.all_gather(part, axis), total)
        inside, total = (start, start)
        for k in reversed(range(size)) if reverse else range(size):
            passed = k > position if reverse else k < position
            total = combine(total, jax.tree.map(lambda part: part[k], pieces))
            inside = jax.tree.map(lambda new, old: jnp.where(passed, new, old), total, inside)
        before = combine(inside, before)
    return before


def by_axis(shard, axes):
    for axis in axes:
        shard = lax.psum(shard, axis)
    return shard


def tile_advance_update(
    acceptance_line_tile,
    lookup_line_tile,
    payload_line_tile,
    source_line_tile,
    reward_array,
    portion_number,
    prior_memory,
    evolving_memory,
):
    element_total, width = acceptance_line_tile.shape
    attention_heads_total, tile_length = (evolving_memory.shape[0], evolving_memory.shape[1])
    hp = lax.Precision.HIGHEST
    logw = -jnp.exp(source_line_tile)
    cum = jnp.cumsum(logw, axis=0)
    before = cum - logw
    carried = (portion_number == prior_memory).astype(jnp.float32)
    query = (acceptance_line_tile * jnp.exp(before)).reshape(
        element_total, attention_heads_total, tile_length
    )
    keyed = (lookup_line_tile * jnp.exp(-cum)).reshape(
        element_total, attention_heads_total, tile_length
    )
    values = payload_line_tile.reshape(element_total, attention_heads_total, tile_length)
    scores = jnp.einsum("jhi,shi->hjs", query, keyed, precision=hp)
    arrangement_sequence = jnp.arange(element_total)
    allowed = (arrangement_sequence[:, None] > arrangement_sequence[None, :]) & (
        portion_number[:, None] == portion_number[None, :]
    )
    scores = jnp.where(allowed[None], scores, 0.0)
    concluding_answer = jnp.einsum("hjs,shc->jhc", scores, values, precision=hp)
    concluding_answer = concluding_answer + carried[:, None, None] * jnp.einsum(
        "jhi,hic->jhc", query, evolving_memory, precision=hp
    )
    immediate_contribution = jnp.sum(
        (acceptance_line_tile * reward_array[None, :] * lookup_line_tile).reshape(
            element_total, attention_heads_total, tile_length
        ),
        axis=2,
    )
    concluding_answer = concluding_answer + immediate_contribution[:, :, None] * values
    keep = (portion_number == portion_number[-1]).astype(jnp.float32)
    ending = (lookup_line_tile * jnp.exp(cum[-1][None, :] - cum) * keep[:, None]).reshape(
        element_total, attention_heads_total, tile_length
    )
    through = jnp.exp(cum[-1]) * (portion_number[-1] == prior_memory).astype(jnp.float32)
    fresh = through.reshape(attention_heads_total, tile_length)[
        :, :, None
    ] * evolving_memory + jnp.einsum("shi,shc->hic", ending, values, precision=hp)
    return (concluding_answer.reshape(element_total, width), fresh)


def compose(earlier, later):
    return (earlier[0] * later[0], later[0][..., None] * earlier[1] + later[1])


def body(
    acceptance_gate,
    lookup_matrix,
    payload_matrix,
    fading_parameter,
    present_reward,
    emitted_cotangent,
    paper_spans,
):
    element_total, width = acceptance_gate.shape
    attention_heads_total = width // HS
    hp = lax.Precision.HIGHEST
    rank = lax.axis_index(SEQ)
    starts = jnp.cumsum(paper_spans) - paper_spans
    positions = rank * element_total - 1 + jnp.arange(element_total + 1)
    seg_all = jnp.sum((starts[None, :] <= positions[:, None]).astype(jnp.int32), axis=1) - 1
    prev_shard = seg_all[0]
    portion_number = seg_all[1:]
    acceptance_line_tile = acceptance_gate.astype(jnp.float32)
    lookup_line_tile = lookup_matrix.astype(jnp.float32)
    payload_line_tile = payload_matrix.astype(jnp.float32)
    rows_dy = emitted_cotangent.astype(jnp.float32)
    logw = -jnp.exp(fading_parameter)
    cum = jnp.cumsum(logw, axis=0)
    before = cum - logw
    carried = (portion_number == prev_shard).astype(jnp.float32)
    through = jnp.exp(cum[-1]) * (portion_number[-1] == prev_shard).astype(jnp.float32)
    keep = (portion_number == portion_number[-1]).astype(jnp.float32)
    ending = (lookup_line_tile * jnp.exp(cum[-1][None, :] - cum) * keep[:, None]).reshape(
        element_total, attention_heads_total, HS
    )
    ends = jnp.einsum(
        "shi,shc->hic",
        ending,
        payload_line_tile.reshape(element_total, attention_heads_total, HS),
        precision=hp,
    ).reshape(width, HS)
    reached = (acceptance_line_tile * jnp.exp(before) * carried[:, None]).reshape(
        element_total, attention_heads_total, HS
    )
    pulls = jnp.einsum(
        "jhi,jhc->hic",
        reached,
        rows_dy.reshape(element_total, attention_heads_total, HS),
        precision=hp,
    ).reshape(width, HS)
    identity = (jnp.ones((width,), jnp.float32), jnp.zeros((width, HS), jnp.float32))
    spare_placeholder, incoming_state = entering((through, ends), SEQ, compose, identity, False)
    spare_placeholder, outgoing = entering((through, pulls), SEQ, compose, identity, True)
    incoming_state = incoming_state.reshape(attention_heads_total, HS, HS)
    outgoing = outgoing.reshape(attention_heads_total, HS, HS)

    def local_result(
        acceptance_division,
        lookup_division,
        payload_division,
        source_division,
        reward_array,
        evolving_memory,
    ):
        concluding_answer, evolving_memory = tile_advance_update(
            acceptance_division,
            lookup_division,
            payload_division,
            source_division,
            reward_array,
            portion_number,
            prev_shard,
            evolving_memory,
        )
        results = [concluding_answer]
        return (jnp.concatenate(results, axis=0), evolving_memory)

    spare_placeholder, adjoint_mapping = jax.vjp(
        local_result,
        acceptance_line_tile,
        lookup_line_tile,
        payload_line_tile,
        fading_parameter,
        present_reward,
        incoming_state,
    )
    derivative_bundle = adjoint_mapping((rows_dy, outgoing))
    reward_cotangent = by_axis(derivative_bundle[4], SEQ)
    return (
        derivative_bundle[0].astype(jnp.bfloat16),
        derivative_bundle[1].astype(jnp.bfloat16),
        derivative_bundle[2].astype(jnp.bfloat16),
        derivative_bundle[3].astype(jnp.bfloat16),
        reward_cotangent,
    )


def solution(mesh):
    split = Mesh(mesh.devices.reshape(4, 4, 4, 2), ("seq_0", "seq_1", "seq_2", "seq_3"))
    in_specs = (P(SEQ, None), P(SEQ, None), P(SEQ, None), P(SEQ, None), P(), P(SEQ, None), P())
    out_specs = (P(SEQ, None), P(SEQ, None), P(SEQ, None), P(SEQ, None), P())
    return jax.shard_map(body, mesh=split, in_specs=in_specs, out_specs=out_specs, check_vma=False)
```

profile of v0, /device:TPU:1, one launch (start us, length us, event | category | flops | bytes accessed | tf_op | source)
XLA Modules:
  0.0 465.6 jit_solution(267794958644595940)
XLA Ops:
  31.0 11.2 %all-gather.23.cloned.1.call-done = f32[2,2048,64]{1,2,0:T(8,128)} async-done(((f32[1,2048,64]{1,2,0:T(8,128)}), f32[2,2048,64]{1,2,0:T(8,128)}) %all-gather.23.cloned.1.call-update) | async-done | bytes 1048592 | tf_op jit(solution)/shard_map/all_gather | solution.py:22
  44.7 9.7 %all-gather.1 = f32[4,1,2048]{2,1,0:T(1,128)S(1)} all-gather(f32[1,1,2048]{2,1,0:T(1,128)S(1)} %get-tuple-element.129), channel_id=1, replica_groups=mesh['seq_0'=4,'seq_1'=4,'seq_2'=4,'seq_3'=2] {'seq_2'}, dimensions={0}, use_global_device_ids=true | all-gather | bytes 40960 | tf_op jit(solution)/shard_map/all_gather | solution.py:22
  54.5 21.8 %all-gather.25.cloned.1.call-done = f32[4,2048,64]{1,2,0:T(8,128)} async-done(((f32[1,2048,64]{1,2,0:T(8,128)}), f32[4,2048,64]{1,2,0:T(8,128)}) %all-gather.25.cloned.1.call-update) | async-done | bytes 2097168 | tf_op jit(solution)/shard_map/all_gather | solution.py:22
  79.5 9.6 %all-gather.4 = f32[4,1,2048]{2,1,0:T(1,128)S(1)} all-gather(f32[1,1,2048]{2,1,0:T(1,128)S(1)} %get-tuple-element.118), channel_id=1, replica_groups=mesh['seq_0'=4,'seq_1'=4,'seq_2'=4,'seq_3'=2] {'seq_1'}, dimensions={0}, use_global_device_ids=true | all-gather | bytes 40960 | tf_op jit(solution)/shard_map/all_gather | solution.py:22
  89.2 21.4 %all-gather.27.cloned.1.call-done = f32[4,2048,64]{1,2,0:T(8,128)} async-done(((f32[1,2048,64]{1,2,0:T(8,128)}), f32[4,2048,64]{1,2,0:T(8,128)}) %all-gather.27.cloned.1.call-update) | async-done | bytes 2097168 | tf_op jit(solution)/shard_map/all_gather | solution.py:22
  119.5 9.8 %all-gather.5 = f32[4,1,2048]{2,1,0:T(1,128)S(1)} all-gather(f32[1,1,2048]{2,1,0:T(1,128)S(1)} %get-tuple-element.113), channel_id=1, replica_groups=mesh['seq_0'=4,'seq_1'=4,'seq_2'=4,'seq_3'=2] {'seq_0'}, dimensions={0}, use_global_device_ids=true | all-gather | bytes 40960 | tf_op jit(solution)/shard_map/all_gather | solution.py:22
  129.3 10.1 %all-gather.2 = f32[4,1,2048]{2,1,0:T(1,128)S(1)} all-gather(f32[1,1,2048]{2,1,0:T(1,128)S(1)} %get-tuple-element.119), channel_id=1, replica_groups=mesh['seq_0'=4,'seq_1'=4,'seq_2'=4,'seq_3'=2] {'seq_1'}, dimensions={0}, use_global_device_ids=true | all-gather | bytes 40960 | tf_op jit(solution)/shard_map/all_gather | solution.py:22
  140.1 9.5 %all-gather.3 = f32[4,1,2048]{2,1,0:T(1,128)S(1)} all-gather(f32[1,1,2048]{2,1,0:T(1,128)S(1)} %get-tuple-element.120), channel_id=1, replica_groups=mesh['seq_0'=4,'seq_1'=4,'seq_2'=4,'seq_3'=2] {'seq_0'}, dimensions={0}, use_global_device_ids=true | all-gather | bytes 40960 | tf_op jit(solution)/shard_map/all_gather | solution.py:22
  189.7 7.4 %add_add_fusion = f32[32,64,64]{1,0,2:T(8,128)S(1)} fusion(f32[32,64,64]{1,0,2:T(8,128)} %squeeze.186, f32[32,64,64]{1,0,2:T(8,128)} %squeeze.185, f32[32,64,64]{1,0,2:T(8,128)} %squeeze.184, f32[32,64,64]{1,0,2:T(8,128)} %squeeze.183, f32[32,64,64]{1,0,2:T(8,128)} %squeeze.182, f32[32,64,64]{1,0,2:T(8,128)} %squeeze.181, f32[32,64,64]{1,0,2:T(8,128)} %squeeze.180, ...), kind=kLoop, calls=%fused_computation.43 | loop fusion | flops 5767168 | bytes 8003598 | tf_op jit(solution)/shard_map/add | solution.py:91
  203.1 4.4 fusion.29
  216.1 18.5 %all-gather.15.cloned.1.call-done = f32[2,2048,64]{1,2,0:T(8,128)} async-done(((f32[1,2048,64]{1,2,0:T(8,128)}), f32[2,2048,64]{1,2,0:T(8,128)}) %all-gather.15.cloned.1.call-update) | async-done | bytes 1048592 | tf_op jit(solution)/shard_map/all_gather | solution.py:22
  237.1 31.6 %all-gather.17.cloned.1.call-done = f32[4,2048,64]{1,2,0:T(8,128)} async-done(((f32[1,2048,64]{1,2,0:T(8,128)}), f32[4,2048,64]{1,2,0:T(8,128)}) %all-gather.17.cloned.1.call-update) | async-done | bytes 2097168 | tf_op jit(solution)/shard_map/all_gather | solution.py:22
  272.0 31.1 %all-gather.19.cloned.1.call-done = f32[4,2048,64]{1,2,0:T(8,128)} async-done(((f32[1,2048,64]{1,2,0:T(8,128)}), f32[4,2048,64]{1,2,0:T(8,128)}) %all-gather.19.cloned.1.call-update) | async-done | bytes 2097168 | tf_op jit(solution)/shard_map/all_gather | solution.py:22
  321.4 9.9 %psum.28 = f32[2048]{0:T(1024)S(1)} all-reduce(f32[2048]{0:T(1024)S(1)} %copy-done.26), channel_id=1, replica_groups=mesh['seq_0'=4,'seq_1'=4,'seq_2'=4,'seq_3'=2] {'seq_0'}, use_global_device_ids=true, to_apply=%region_10.11 | all-reduce | flops 2048 | bytes 16384 | tf_op jit(solution)/shard_map/psum | solution.py:34
  331.3 6.7 %psum.29 = f32[2048]{0:T(1024)S(1)} all-reduce(f32[2048]{0:T(1024)S(1)} %psum.28), channel_id=1, replica_groups=mesh['seq_0'=4,'seq_1'=4,'seq_2'=4,'seq_3'=2] {'seq_1'}, use_global_device_ids=true, to_apply=%region_11.12 | all-reduce | flops 2048 | bytes 16384 | tf_op jit(solution)/shard_map/psum | solution.py:34
  338.0 8.6 %psum.30 = f32[2048]{0:T(1024)S(1)} all-reduce(f32[2048]{0:T(1024)S(1)} %psum.29), channel_id=1, replica_groups=mesh['seq_0'=4,'seq_1'=4,'seq_2'=4,'seq_3'=2] {'seq_2'}, use_global_device_ids=true, to_apply=%region_12.13 | all-reduce | flops 2048 | bytes 16384 | tf_op jit(solution)/shard_map/psum | solution.py:34
  346.6 8.8 %psum.31 = f32[2048]{0:T(1024)} all-reduce(f32[2048]{0:T(1024)S(1)} %psum.30), channel_id=1, replica_groups=mesh['seq_0'=4,'seq_1'=4,'seq_2'=4,'seq_3'=2] {'seq_3'}, use_global_device_ids=true, to_apply=%region_13.14 | all-reduce | flops 2048 | bytes 16384 | tf_op jit(solution)/shard_map/psum | solution.py:34
  355.4 4.4 convolution_bitcast_fusion
  359.8 4.9 %fusion.65 = f32[32,128,128]{2,1,0:T(8,128)} fusion(f32[128,32,64]{0,2,1:T(8,128)S(1)} %bitcast.187, f32[128,32,64]{0,2,1:T(8,128)S(1)} %bitcast.184), kind=kOutput, calls=%fused_computation.159 | convolution fusion | flops 402653184 | bytes 4194304 | tf_op jit(solution)/shard_map/jvp(jhi,shi->hjs)/dot_general | solution.py:62
  387.4 5.9 %multiply_reduce_fusion = f32[2048]{0:T(1024)S(1)} fusion(f32[1,2048,64]{1,2,0:T(8,128)} %get-tuple-element.100, f32[1,2048,64]{1,2,0:T(8,128)} %get-tuple-element.89, f32[1,2048,64]{1,2,0:T(8,128)} %get-tuple-element.84, f32[1,2048,64]{1,2,0:T(8,128)S(1)} %copy-done.12, f32[1,2048,64]{1,2,0:T(8,128)} %get-tuple-element.75, ...), kind=kLoop, calls=%fused_computation.60 | loop fusion | flops 10221568 | bytes 14901276 | tf_op jit(solution)/shard_map/transpose(jvp())/reduce_sum | solution.py:84
  403.5 7.5 %add_add_fusion.1 = f32[32,64,64]{1,0,2:T(8,128)S(1)} fusion(f32[32,64,64]{1,0,2:T(8,128)} %squeeze.168, f32[32,64,64]{1,0,2:T(8,128)} %squeeze.167, f32[32,64,64]{1,0,2:T(8,128)} %squeeze.166, f32[32,64,64]{1,0,2:T(8,128)} %squeeze.165, f32[32,64,64]{1,0,2:T(8,128)} %squeeze.164, f32[32,64,64]{1,0,2:T(8,128)} %squeeze.163, f32[32,64,64]{1,0,2:T(8,128)} %squeeze.162, ...), kind=kLoop, calls=%fused_computation.50 | loop fusion | flops 5767168 | bytes 8003598 | tf_op jit(solution)/shard_map/add | solution.py:91
  413.3 5.1 %fusion.8 = f32[32,128,64]{1,2,0:T(8,128)} fusion(f32[32,128,64]{1,2,0:T(8,128)S(1)} %fusion.26, f32[128,32,64]{0,2,1:T(8,128)S(1)} %bitcast.185, f32[32,128,128]{2,1,0:T(8,128)S(1)} %copy-done.1, pred[128,128]{1,0:T(8,128)(4,1)S(1)} %fusion.49), kind=kOutput, calls=%fused_computation.21 | convolution fusion | flops 403439616 | bytes 5259264 | tf_op jit(solution)/shard_map/transpose(jvp(jhi,shi->hjs))/dot_general | solution.py:62
  421.1 5.3 %fusion.35 = (f32[128,2048]{1,0:T(8,128)}, bf16[128,2048]{1,0:T(8,128)(2,1)}, bf16[128,2048]{1,0:T(8,128)(2,1)}, f32[128,2048]{1,0:T(8,128)}) fusion(f32[128,2048]{1,0:T(8,128)} %copy.81, bf16[128,2048]{1,0:T(8,128)(2,1)} %param.8, f32[1,2048]{1,0:T(1,128)S(1)} %bitcast.254, f32[1,2048]{1,0:T(1,128)S(1)} %exponential_multiply_fusion, ...), kind=kLoop, calls=%fused_computation.40 | loop fusion | flops 8388608 | bytes 10519040 | tf_op jit(solution)/shard_map/transpose(jvp())/add_any | solution.py:53
  435.4 20.1 %reduce_window_sum.42 = f32[128,2048]{1,0:T(8,128)} reduce-window(f32[128,2048]{1,0:T(8,128)} %get-tuple-element.63, f32[]{:T(128)} %constant.20.clone.1), window={size=128x1 pad=0_127x0_0}, to_apply=%region_8.9 | reduce-window | flops 33292288 | bytes 2097156 | tf_op jit(solution)/shard_map/transpose(jvp(jit(cumsum)))/reduce_window_sum | solution.py:52
  (225 shorter events, 166.0 us)
Async XLA Ops:
  7.2 35.0 %all-gather.23.cloned.1.call-start = ((), (), s32[]{:S(2)}) async-start(), calls=%async_computation.4 | async-start | bytes 1572864 | tf_op jit(solution)/shard_map/all_gather | solution.py:22
  26.7 49.6 %all-gather.25.cloned.1.call-start = ((), (), s32[]{:S(2)}) async-start(), calls=%async_computation.5 | async-start | bytes 2621440 | tf_op jit(solution)/shard_map/all_gather | solution.py:22
  44.6 65.9 %all-gather.27.cloned.1.call-start = ((), (), s32[]{:S(2)}) async-start(), calls=%async_computation.6 | async-start | bytes 2621440 | tf_op jit(solution)/shard_map/all_gather | solution.py:22
  79.4 97.6 %all-gather.29.cloned.1.call-start = ((), (), s32[]{:S(2)}) async-start(), calls=%async_computation.7 | async-start | bytes 2621440 | tf_op jit(solution)/shard_map/all_gather | solution.py:22
  113.7 121.0 %all-gather.15.cloned.1.call-start = ((), (), s32[]{:S(2)}) async-start(), calls=%async_computation | async-start | bytes 1572864 | tf_op jit(solution)/shard_map/all_gather | solution.py:22
  182.3 7.4 %copy-start.19 = (f32[32,64]{1,0:T(8,128)S(1)}, f32[32,64]{1,0:T(8,128)}, u32[]{:S(2)}) copy-start(f32[32,64]{1,0:T(8,128)} %get-tuple-element.144) | copy-start | bytes 24580
  216.0 52.7 %all-gather.17.cloned.1.call-start = ((), (), s32[]{:S(2)}) async-start(), calls=%async_computation.1 | async-start | bytes 2621440 | tf_op jit(solution)/shard_map/all_gather | solution.py:22
  237.1 66.0 %all-gather.19.cloned.1.call-start = ((), (), s32[]{:S(2)}) async-start(), calls=%async_computation.2 | async-start | bytes 2621440 | tf_op jit(solution)/shard_map/all_gather | solution.py:22
  271.9 115.5 %all-gather.21.cloned.1.call-start = ((), (), s32[]{:S(2)}) async-start(), calls=%async_computation.3 | async-start | bytes 2621440 | tf_op jit(solution)/shard_map/all_gather | solution.py:22
  313.1 8.3 %copy-start.26 = (f32[2048]{0:T(1024)S(1)}, f32[2048]{0:T(1024)}, u32[]{:S(2)}) copy-start(f32[2048]{0:T(1024)} %get-tuple-element.25) | copy-start | bytes 24580
  359.8 7.4 %copy-start.13 = (f32[1,2048,64]{1,2,0:T(8,128)S(1)}, f32[1,2048,64]{1,2,0:T(8,128)}, u32[]{:S(2)}) copy-start(f32[1,2048,64]{1,2,0:T(8,128)} %get-tuple-element.102) | copy-start | bytes 1572868
  368.6 7.4 %copy-start.14 = (f32[1,2048,64]{1,2,0:T(8,128)S(1)}, f32[1,2048,64]{1,2,0:T(8,128)}, u32[]{:S(2)}) copy-start(f32[1,2048,64]{1,2,0:T(8,128)} %get-tuple-element.93) | copy-start | bytes 1572868
  379.9 7.5 %copy-start.12 = (f32[1,2048,64]{1,2,0:T(8,128)S(1)}, f32[1,2048,64]{1,2,0:T(8,128)}, u32[]{:S(2)}) copy-start(f32[1,2048,64]{1,2,0:T(8,128)} %get-tuple-element.97) | copy-start | bytes 1572868
  379.9 7.5 %copy-start.20 = (f32[1,1,2048]{2,1,0:T(1,128)S(1)}, f32[1,1,2048]{2,1,0:T(1,128)}, u32[]{:S(2)}) copy-start(f32[1,1,2048]{2,1,0:T(1,128)} %get-tuple-element.106) | copy-start | bytes 24580
  379.9 7.5 %copy-start.21 = (f32[1,1,2048]{2,1,0:T(1,128)S(1)}, f32[1,1,2048]{2,1,0:T(1,128)}, u32[]{:S(2)}) copy-start(f32[1,1,2048]{2,1,0:T(1,128)} %get-tuple-element.107) | copy-start | bytes 24580
  379.9 7.5 %copy-start.22 = (f32[1,1,2048]{2,1,0:T(1,128)S(1)}, f32[1,1,2048]{2,1,0:T(1,128)}, u32[]{:S(2)}) copy-start(f32[1,1,2048]{2,1,0:T(1,128)} %get-tuple-element.108) | copy-start | bytes 24580
  379.9 7.5 %copy-start.23 = (f32[1,1,2048]{2,1,0:T(1,128)S(1)}, f32[1,1,2048]{2,1,0:T(1,128)}, u32[]{:S(2)}) copy-start(f32[1,1,2048]{2,1,0:T(1,128)} %get-tuple-element.136) | copy-start | bytes 24580
  379.9 7.5 %copy-start.24 = (f32[1,1,2048]{2,1,0:T(1,128)S(1)}, f32[1,1,2048]{2,1,0:T(1,128)}, u32[]{:S(2)}) copy-start(f32[1,1,2048]{2,1,0:T(1,128)} %get-tuple-element.137) | copy-start | bytes 24580
  379.9 7.5 %copy-start.25 = (f32[1,1,2048]{2,1,0:T(1,128)S(1)}, f32[1,1,2048]{2,1,0:T(1,128)}, u32[]{:S(2)}) copy-start(f32[1,1,2048]{2,1,0:T(1,128)} %get-tuple-element.138) | copy-start | bytes 24580
  397.0 6.4 %copy-start.16 = (f32[32,64]{1,0:T(8,128)S(1)}, f32[32,64]{1,0:T(8,128)}, u32[]{:S(2)}) copy-start(f32[32,64]{1,0:T(8,128)} %broadcast_multiply_fusion.6) | copy-start | bytes 24580
  397.0 6.4 %copy-start.17 = (f32[32,64]{1,0:T(8,128)S(1)}, f32[32,64]{1,0:T(8,128)}, u32[]{:S(2)}) copy-start(f32[32,64]{1,0:T(8,128)} %get-tuple-element.146) | copy-start | bytes 24580
  397.0 6.4 %copy-start.18 = (f32[32,64]{1,0:T(8,128)S(1)}, f32[32,64]{1,0:T(8,128)}, u32[]{:S(2)}) copy-start(f32[32,64]{1,0:T(8,128)} %get-tuple-element.147) | copy-start | bytes 24580
  403.5 7.5 %copy-start.40 = (f32[128]{0:T(128)S(1)}, f32[128]{0:T(128)}, u32[]{:S(2)}) copy-start(f32[128]{0:T(128)} %copy-done.39) | copy-start | bytes 1540
  403.5 9.8 %copy-start.5 = (f32[128,2048]{0,1:T(8,128)S(1)}, f32[128,2048]{0,1:T(8,128)}, u32[]{:S(2)}) copy-start(f32[128,2048]{0,1:T(8,128)} %copy.73) | copy-start | bytes 3145732
  (27 other events, 88.7 us)
Sparse Core Ops, SparseCore 0:
  26.8 15.3 all-gather.22
  44.8 31.5 all-gather.24
  79.5 30.9 all-gather.26
  113.8 30.7 all-gather.28
  216.1 18.4 all-gather.14
  237.2 31.5 all-gather.16
  272.0 30.9 all-gather.18
  306.3 30.9 all-gather.20
where the time goes:
time: 473 us; the launch traced here: 466 us
  waiting for transfers between devices  136 us (29%)
  local copies, waits for them, and re-layouts  106 us (22%)
  other arithmetic  89.9 us (19%)
  blocking collectives  85.6 us (18%)
  matrix products  31.6 us (7%)
  between operations  16.4 us (3%)
    all_gather x8, waiting for transfers between devices, entering(): pieces = jax.tree.map(lambda part: lax.all_gather(part, axis), total)  136 us
    squeeze x42, local copies, waits for them, and re-layouts, entering(): total = combine(total, jax.tree.map(lambda part: part[k], pieces))  66.9 us
    all_gather x6, blocking collectives, entering(): pieces = jax.tree.map(lambda part: lax.all_gather(part, axis), total)  51.6 us
    psum x4, blocking collectives, by_axis(): shard = lax.psum(shard, axis)  34 us
    add x8, other arithmetic, compose(): return (earlier[0] * later[0], later[0][..., None] * earlier[1] + later[1])  32 us
    another operation x1, other arithmetic, tile_advance_update(): cum = jnp.cumsum(logw, axis=0)  20.1 us
    dot_general x3, matrix products, tile_advance_update(): scores = jnp.einsum('jhi,shi->hjs', query, keyed, precision=hp)  13 us
  transfers between devices with their start and end apart: 8, of which 6 were waited for; matrix products, arithmetic and copies ran while one was open for 17% of the time, Pallas kernels for 0%

commit v1 on v0

v1 whole, which is shorter than its diff:
```python
import jax
import jax.numpy as jnp
from jax import lax
from jax.experimental import pallas as pl
from jax.experimental.pallas import tpu as pltpu
from jax.sharding import PartitionSpec as P

HS = 64
LANES = 128
TOK = 128
STATE_ROWS = 8
ROWS = 24
PAIRS = 4
F32 = jnp.float32
BF16 = jnp.bfloat16

NN = (((1,), (0,)), ((), ()))
NT = (((1,), (1,)), ((), ()))
TN = (((0,), (0,)), ((), ()))


def dot(a, b, dims):
    return lax.dot_general(a, b, dims, preferred_element_type=F32)


def halves(x):
    high = x.astype(BF16)
    return high, (x - high.astype(F32)).astype(BF16)


def head_masks():
    lane = lax.broadcasted_iota(jnp.int32, (1, LANES), 1)
    return (lane < HS).astype(F32).astype(BF16), (lane >= HS).astype(F32).astype(BF16)


def by_head(x, masks):
    return jnp.concatenate([x * masks[0], x * masks[1]], axis=0)


def side_by_side(x):
    return jnp.concatenate([x[:TOK], x[TOK:]], axis=1)


def cat(*parts, axis):
    return jnp.concatenate(parts, axis=axis)


def square(n=TOK):
    row = lax.broadcasted_iota(jnp.int32, (n, n), 0)
    return row, lax.broadcasted_iota(jnp.int32, (n, n), 1)


def ones_by_head():
    row, col = square()
    same = ((row < HS) == (col < HS)).astype(F32).astype(BF16)
    return cat(same, same, axis=0)


def head_sums(x, ones):
    high, low = halves(x)
    return dot(cat(high, low, axis=1), ones, NN)


def segments(spans, base):
    ndocs = spans.shape[1]
    row, col = square(ndocs)
    ends_down = jnp.sum(jnp.where(col <= row, spans, 0.0), axis=1, keepdims=True)
    spans_down = jnp.sum(jnp.where(col == row, spans, 0.0), axis=1, keepdims=True)
    ends = jnp.sum(jnp.where(row <= col, spans_down, 0.0), axis=0, keepdims=True)
    across = (base + lax.broadcasted_iota(jnp.int32, (1, TOK), 1)).astype(F32)
    down = (base + lax.broadcasted_iota(jnp.int32, (TOK, 1), 0)).astype(F32)
    seg_across = jnp.sum(jnp.where(ends_down <= across, 1.0, 0.0), axis=0, keepdims=True)
    seg_down = jnp.sum(jnp.where(ends <= down, 1.0, 0.0), axis=1, keepdims=True)
    prev = jnp.sum(jnp.where(ends <= down[:1] - 1.0, 1.0, 0.0), axis=1, keepdims=True)
    return seg_across, seg_down, jnp.where(down[:1] > 0.0, prev, -1.0)


def summary_kernel(rank, spans, r, k, v, g, x, out, cum_out, masks_out, keep, carried, passes):
    @pl.when(pl.program_id(0) == 0)
    def _():
        seg_across, seg_down, prev = segments(spans[...].astype(F32), rank[0] * TOK)
        row, col = square()
        same = seg_down == seg_across
        last = seg_down[TOK - 1 :]
        keep[...] = jnp.broadcast_to((seg_down == last).astype(F32), (TOK, LANES))
        carried[...] = jnp.broadcast_to((seg_down == prev).astype(F32), (TOK, LANES))
        passes[...] = jnp.broadcast_to((last == prev).astype(F32), passes.shape)
        masks_out[0] = (same & (row > col)).astype(F32)
        masks_out[1] = (same & (row < col)).astype(F32)
        masks_out[2] = keep[...]
        masks_out[3] = carried[...]

    row, col = square()
    lower = (row >= col).astype(F32).astype(BF16)
    lower = cat(lower, lower, axis=1)
    ones = ones_by_head()
    lane = lax.broadcasted_iota(jnp.int32, (HS, LANES), 1)
    for pair in range(PAIRS):
        at = slice(pair * LANES, (pair + 1) * LANES)
        logw = -jnp.exp(x[:, at])
        cum = dot(lower, cat(*halves(logw), axis=0), NN)
        cum_out[:, at] = cum
        last = cum[TOK - 1 :]
        rp, kp = r[:, at].astype(F32), k[:, at].astype(F32)
        ending = cat(*halves(kp * jnp.exp(last - cum) * keep[...]), axis=1)
        reached = cat(*halves(rp * jnp.exp(cum - logw) * carried[...]), axis=1)
        ends, pulls = dot(v[:, at], ending, TN), dot(g[:, at], reached, TN)
        bonus = head_sums(g[:, at].astype(F32) * v[:, at].astype(F32), ones)
        bonus = jnp.sum(rp * kp * bonus, axis=0, keepdims=True)
        through = jnp.exp(last) * passes[:1]
        peers = slice(pair * STATE_ROWS, (pair + 1) * STATE_ROWS)
        for place, both in ((0, ends), (1, pulls)):
            both = both[:, :LANES] + both[:, LANES:]
            state = jnp.where(lane < HS, both[:HS], both[HS:])
            out[peers, place * STATE_ROWS : (place + 1) * STATE_ROWS] = state.reshape(
                HS // STATE_ROWS, STATE_ROWS, LANES
            )
        rest = cat(through, bonus, jnp.zeros((6, LANES), F32), axis=0)
        out[peers, 2 * STATE_ROWS :] = jnp.broadcast_to(rest[None], (STATE_ROWS, 8, LANES))


def scan_kernel(got, out):
    shards = got.shape[0]
    state = jnp.zeros((STATE_ROWS, LANES), F32)
    bonus = jnp.zeros((8, LANES), F32)
    for at in range(shards):
        out[at, :STATE_ROWS] = state
        rest = got[at, 2 * STATE_ROWS :]
        state = rest[:1] * state + got[at, :STATE_ROWS]
        bonus = bonus + rest
    state = jnp.zeros((STATE_ROWS, LANES), F32)
    for at in reversed(range(shards)):
        out[at, STATE_ROWS : 2 * STATE_ROWS] = state
        state = got[at, 2 * STATE_ROWS : 2 * STATE_ROWS + 1] * state + got[at, STATE_ROWS : 2 * STATE_ROWS]
        out[at, 2 * STATE_ROWS :] = bonus


def inside_kernel(r, k, v, g, x, cum_in, u, masks, dr, dk, dv, dl):
    heads = head_masks()
    ones = ones_by_head()
    row, col = square()
    after = (row < col).astype(F32).astype(BF16)
    onward = -((row <= col).astype(F32).astype(BF16))
    sums = cat(after, onward, axis=1)
    allowed = cat(masks[0], masks[0], axis=0)
    allowed_t = cat(masks[1], masks[1], axis=0)
    for pair in range(PAIRS):
        at = slice(pair * LANES, (pair + 1) * LANES)
        rb, kb, vb, gb = r[:, at], k[:, at], v[:, at], g[:, at]
        rp, kp, vp, gp = (part.astype(F32) for part in (rb, kb, vb, gb))
        cum = cum_in[:, at]
        middle = 0.5 * cum[TOK - 1 :]
        scale_r = jnp.exp(cum + jnp.exp(x[:, at]) - middle)
        scale_k = jnp.exp(middle - cum)
        rh, rl = halves(rp * scale_r)
        kh, kl = halves(kp * scale_k)
        rh2, rl2, kh2, kl2 = (by_head(part, heads) for part in (rh, rl, kh, kl))
        g2, v2 = by_head(gb, heads), by_head(vb, heads)
        scores = dot(cat(kh2, kl2, axis=1), cat(rh, rh, axis=1), NT) + dot(kh2, rl, NT)
        scores = jnp.where(allowed_t > 0.0, scores, 0.0)
        sh, sl = halves(side_by_side(scores))
        direct = u[:, at]
        dv[:, at] = dot(sh, g2, NN) + dot(sl, g2, NN) + head_sums(rp * direct * kp, ones) * gp
        pull = side_by_side(dot(g2, vb, NT) * allowed)
        pull_t = side_by_side(dot(v2, gb, NT) * allowed_t)
        ph, plow = halves(pull)
        th, tl = halves(pull_t)
        dri = scale_r * (dot(ph, kh2, NN) + dot(ph, kl2, NN) + dot(plow, kh2, NN))
        dki = scale_k * (dot(th, rh2, NN) + dot(th, rl2, NN) + dot(tl, rh2, NN))
        own = direct * head_sums(gp * vp, ones)
        dr[:, at] = dri + own * kp
        dk[:, at] = dki + own * rp
        high, low = halves(cat(rp * dri, kp * dki, axis=0))
        dl[:, at] = dot(sums, high, NN) + dot(sums, low, NN)


def final_kernel(r, k, v, g, x, cum_in, masks, dri, dki, dvi, dli, got, dr, dk, dv, dx, du):
    heads = head_masks()
    row, col = square()
    after = (row < col).astype(F32).astype(BF16)
    earlier = (row > col).astype(F32).astype(BF16)
    sums = cat(after, earlier, axis=1)
    for pair in range(PAIRS):
        at = slice(pair * LANES, (pair + 1) * LANES)
        peers = slice(pair * STATE_ROWS, (pair + 1) * STATE_ROWS)
        state = got[peers, :STATE_ROWS].reshape(HS, LANES)
        dstate = got[peers, STATE_ROWS : 2 * STATE_ROWS].reshape(HS, LANES)
        du[:, at] = got[pair * STATE_ROWS, 2 * STATE_ROWS + 1 : 2 * STATE_ROWS + 2]
        rp, kp = r[:, at].astype(F32), k[:, at].astype(F32)
        cum = cum_in[:, at]
        last = cum[TOK - 1 :]
        rate = jnp.exp(x[:, at])
        kd = jnp.exp(last - cum) * masks[2]
        rd = jnp.exp(cum + rate) * masks[3]
        sh, sl = (by_head(part, heads) for part in halves(state))
        dh, dlow = (by_head(part, heads) for part in halves(dstate))
        drs = rd * (dot(g[:, at], sh, NN) + dot(g[:, at], sl, NN))
        dks = kd * (dot(v[:, at], dh, NN) + dot(v[:, at], dlow, NN))
        eh, el = halves(kp * kd)
        dvs = dot(eh, dh, NT) + dot(eh, dlow, NT) + dot(el, dh, NT)
        dr[:, at] = (dri[:, at] + drs).astype(BF16)
        dk[:, at] = (dki[:, at] + dks).astype(BF16)
        dv[:, at] = (dvi[:, at] + dvs).astype(BF16)
        high, low = halves(cat(rp * drs, kp * dks, axis=0))
        both = masks[2][TOK - 1 :] * masks[3][TOK - 1 :]
        across = jnp.exp(last) * both * jnp.sum(state * dstate, axis=0, keepdims=True)
        grad = dli[:, at] + dot(sums, high, NN) + dot(sums, low, NN) + across
        dx[:, at] = (-rate * grad).astype(BF16)


def body(r, k, v, x, u, g, spans):
    tokens, width = r.shape
    npairs = width // LANES
    peers = lax.axis_size("seq")
    steps = npairs // PAIRS
    part = PAIRS * LANES
    rank = lax.axis_index("seq").astype(jnp.int32).reshape(1)
    wide = pl.BlockSpec((TOK, part), lambda i, *_: (0, i))
    thin = pl.BlockSpec((1, part), lambda i, *_: (0, i))
    sent = pl.BlockSpec((PAIRS * STATE_ROWS, ROWS, LANES), lambda i, *_: (i, 0, 0))
    fixed = pl.BlockSpec((4, TOK, LANES), lambda i, *_: (0, 0, 0))
    full = jax.ShapeDtypeStruct((tokens, width), F32)
    rounded = jax.ShapeDtypeStruct((tokens, width), BF16)
    packet = jax.ShapeDtypeStruct((peers, ROWS, LANES), F32)

    summaries, cum, masks = pl.pallas_call(
        summary_kernel,
        grid_spec=pltpu.PrefetchScalarGridSpec(
            num_scalar_prefetch=1,
            grid=(steps,),
            in_specs=[pl.BlockSpec((1, spans.shape[0]), lambda i, *_: (0, 0))] + [wide] * 5,
            out_specs=[sent, wide, fixed],
            scratch_shapes=[
                pltpu.VMEM((TOK, LANES), F32),
                pltpu.VMEM((TOK, LANES), F32),
                pltpu.VMEM((8, LANES), F32),
            ],
        ),
        out_shape=[packet, full, jax.ShapeDtypeStruct((4, TOK, LANES), F32)],
        name="summary",
        cost_estimate=pl.CostEstimate(flops=10**9, bytes_accessed=6 * 10**6, transcendentals=10**6),
    )(rank, spans.reshape(1, -1), r, k, v, g, x)
    got = lax.all_to_all(summaries, "seq", 0, 0, tiled=True)
    dri, dki, dvi, dli = pl.pallas_call(
        inside_kernel,
        grid=(steps,),
        in_specs=[wide] * 6 + [thin, fixed],
        out_specs=[wide] * 4,
        out_shape=[full] * 4,
        name="inside",
        cost_estimate=pl.CostEstimate(flops=10**10, bytes_accessed=10**7, transcendentals=10**6),
    )(r, k, v, g, x, cum, u.reshape(1, -1), masks)
    states = pl.pallas_call(
        scan_kernel,
        out_shape=packet,
        name="scan",
        cost_estimate=pl.CostEstimate(flops=10**6, bytes_accessed=3 * 10**6, transcendentals=0),
    )(got)
    returned = lax.all_to_all(states, "seq", 0, 0, tiled=True)
    dr, dk, dv, dx, du = pl.pallas_call(
        final_kernel,
        grid=(steps,),
        in_specs=[wide] * 6 + [fixed] + [wide] * 4 + [sent],
        out_specs=[wide] * 4 + [thin],
        out_shape=[rounded] * 4 + [jax.ShapeDtypeStruct((1, width), F32)],
        name="final",
        cost_estimate=pl.CostEstimate(flops=10**9, bytes_accessed=10**7, transcendentals=10**6),
    )(r, k, v, g, x, cum, masks, dri, dki, dvi, dli, returned)
    return dr, dk, dv, dx, du.reshape(width)


def solution(mesh):
    split, whole = P("seq", None), P()
    return jax.shard_map(
        body,
        mesh=mesh,
        in_specs=(split, split, split, split, whole, split, whole),
        out_specs=(split, split, split, split, whole),
        check_vma=False,
    )
```

time: 473 us -> 85.5 us (0.18); the launches traced: 466 us -> 85.1 us
  waiting for transfers between devices: 136 us -> 10.7 us
  local copies, waits for them, and re-layouts: 106 us -> 1.15 us
  other arithmetic: 89.9 us -> 0 us
  blocking collectives: 85.6 us -> 36.2 us
  Pallas kernels: 0 us -> 31.7 us
  matrix products: 31.6 us -> 0 us
  between operations: 16.4 us -> 0.65 us
    all_gather x8 -> x0, waiting for transfers between devices: 136 us -> none  [entering(): pieces = jax.tree.map(lambda part: lax.all_gather(part, axis), total)]
    squeeze x42 -> x0, local copies, waits for them, and re-layouts: 66.9 us -> none  [entering(): total = combine(total, jax.tree.map(lambda part: part[k], pieces))]
    all_gather x6 -> x0, blocking collectives: 51.6 us -> none  [entering(): pieces = jax.tree.map(lambda part: lax.all_gather(part, axis), total)]
    all_to_all x0 -> x1, blocking collectives: none -> 36.2 us  [body(): got = lax.all_to_all(summaries, 'seq', 0, 0, tiled=True)]
    psum x4 -> x0, blocking collectives: 34 us -> none  [by_axis(): shard = lax.psum(shard, axis)]
    add x9 -> x0, other arithmetic: 32 us -> none  [the longest x8 32 us: compose(): return (earlier[0] * later[0], later[0][..., None] * earlier[1] + later[1])]
    pallas_call x0 -> x4, Pallas kernels: none -> 31.7 us  [the longest x1 14 us: body(): pl.pallas_call(inside_kernel, grid=(steps,), in_specs=[wide] * 6 + [thin,...]
    dot_general x10 -> x0, matrix products: 31.6 us -> none  [the longest x3 13 us: tile_advance_update(): scores = jnp.einsum('jhi,shi->hjs', query, keyed, precision=hp)]
  transfers between devices with their start and end apart: 8 -> 1, of which waited for: 6 -> 1; matrix products, arithmetic and copies ran while one was open for 17% -> 0% of each run, Pallas kernels for 0% -> 16%
where the time goes in v1:
time: 85.5 us; the launch traced here: 85.1 us
  blocking collectives  36.2 us (42%)
  Pallas kernels  31.7 us (37%)
  waiting for transfers between devices  10.7 us (13%)
  starting transfers between devices  4.69 us (5%)
  local copies, waits for them, and re-layouts  1.15 us (1%)
    all_to_all x1, blocking collectives, body(): got = lax.all_to_all(summaries, 'seq', 0, 0, tiled=True)  36.2 us
    pallas_call x1, Pallas kernels, body(): pl.pallas_call(inside_kernel, grid=(steps,), in_specs=[wide] * 6 + [thin,...  14 us
    all_to_all x1, waiting for transfers between devices, body(): returned = lax.all_to_all(states, 'seq', 0, 0, tiled=True)  10.7 us
    pallas_call x1, Pallas kernels, body(): pl.pallas_call(final_kernel, grid=(steps,), in_specs=[wide] * 6 + [fixed]...  8.07 us
    pallas_call x1, Pallas kernels, body(): pl.pallas_call(summary_kernel, grid_spec=pltpu.PrefetchScalarGridSpec(num...  6.77 us
    all_to_all x1, starting transfers between devices, body(): returned = lax.all_to_all(states, 'seq', 0, 0, tiled=True)  4.69 us
    pallas_call x1, Pallas kernels, body(): pl.pallas_call(scan_kernel, out_shape=packet, name='scan', cost_estimate=...  2.86 us
  transfers between devices with their start and end apart: 1, of which 1 were waited for; matrix products, arithmetic and copies ran while one was open for 0% of the time, Pallas kernels for 16%

profile of v1, /device:TPU:1, one launch (start us, length us, event | category | flops | bytes accessed | tf_op | source)
XLA Modules:
  0.0 85.1 jit_solution(13187948521624619302)
XLA Ops:
  0.6 6.8 %summary.1 = (f32[128,24,128]{2,1,0:T(8,128)}, f32[128,2048]{1,0:T(8,128)}, f32[4,128,128]{2,1,0:T(8,128)}) custom-call(s32[1]{0:T(128)} %bitcast.rank, s32[1,256]{1,0:T(1,128)} %bitcast.6, bf16[128,2048]{1,0:T(8,128)(2,1)} %r.5, bf16[128,2048]{1,0:T(8,128)(2,1)} %k.5, bf16[128,2048]{1,0:T(8,128)(2,1)} %v.5, bf16[128,2048]{1,0:T(8,128)(2,1)} %g.5, f32[128,2048]{1,0:T(8,128)} %x.5), custom_call_target="tpu_custom_call" | custom-call | flops 1000000000 | bytes 6000000 | tf_op jit(solution)/shard_map/summary/pallas_call | solution.py:226
  7.4 36.2 %all_to_all.10.got = f32[128,24,128]{2,1,0:T(8,128)} all-to-all(f32[128,24,128]{2,1,0:T(8,128)} %get-tuple-element.23), channel_id=1, replica_groups=mesh['seq'=128] {'seq'}, dimensions={0} | all-to-all | bytes 3145728 | tf_op jit(solution)/shard_map/all_to_all | solution.py:243
  43.6 2.9 %scan.1 = f32[128,24,128]{2,1,0:T(8,128)} custom-call(f32[128,24,128]{2,1,0:T(8,128)} %all_to_all.10.got), custom_call_target="tpu_custom_call" | custom-call | flops 1000000 | bytes 3000000 | tf_op jit(solution)/shard_map/scan/pallas_call | solution.py:253
  46.4 4.7 %all-to-all-start.1 = ((f32[128,24,128]{2,1,0:T(8,128)}), f32[128,24,128]{2,1,0:T(8,128)S(1)}, u32[]{:S(2)}, u32[]{:S(2)}) async-start(f32[128,24,128]{2,1,0:T(8,128)} %scan.1), calls=%async_computation.1 | async-start | bytes 3145728 | tf_op jit(solution)/shard_map/all_to_all | solution.py:259
  51.1 14.0 %inside.1 = (f32[128,2048]{1,0:T(8,128)}, f32[128,2048]{1,0:T(8,128)}, f32[128,2048]{1,0:T(8,128)}, f32[128,2048]{1,0:T(8,128)}) custom-call(bf16[128,2048]{1,0:T(8,128)(2,1)} %r.5, bf16[128,2048]{1,0:T(8,128)(2,1)} %k.5, bf16[128,2048]{1,0:T(8,128)(2,1)} %v.5, bf16[128,2048]{1,0:T(8,128)(2,1)} %g.5, f32[128,2048]{1,0:T(8,128)} %x.5, ...), custom_call_target="tpu_custom_call" | custom-call | flops 10000000000 | bytes 10000000 | tf_op jit(solution)/shard_map/inside/pallas_call | solution.py:244
  65.1 10.7 %all-to-all-done.1.got = f32[128,24,128]{2,1,0:T(8,128)S(1)} async-done(((f32[128,24,128]{2,1,0:T(8,128)}), f32[128,24,128]{2,1,0:T(8,128)S(1)}, u32[]{:S(2)}, u32[]{:S(2)}) %all-to-all-start.1) | async-done | bytes 1572896 | tf_op jit(solution)/shard_map/all_to_all | solution.py:259
  75.9 0.0 copy-start
  75.9 1.1 %copy-done = f32[128,24,128]{2,1,0:T(8,128)} copy-done((f32[128,24,128]{2,1,0:T(8,128)}, f32[128,24,128]{2,1,0:T(8,128)S(1)}, u32[]{:S(2)}) %copy-start) | copy-done | bytes 1572888
  77.0 8.1 %final.1 = (bf16[128,2048]{1,0:T(8,128)(2,1)}, bf16[128,2048]{1,0:T(8,128)(2,1)}, bf16[128,2048]{1,0:T(8,128)(2,1)}, bf16[128,2048]{1,0:T(8,128)(2,1)}, f32[1,2048]{1,0:T(1,128)}) custom-call(bf16[128,2048]{1,0:T(8,128)(2,1)} %r.5, bf16[128,2048]{1,0:T(8,128)(2,1)} %k.5, bf16[128,2048]{1,0:T(8,128)(2,1)} %v.5, bf16[128,2048]{1,0:T(8,128)(2,1)} %g.5, ...), custom_call_target="tpu_custom_call" | custom-call | flops 1000000000 | bytes 10000000 | tf_op jit(solution)/shard_map/final/pallas_call | solution.py:260
Async XLA Ops:
  46.4 29.4 %all-to-all-start.1 = ((f32[128,24,128]{2,1,0:T(8,128)}), f32[128,24,128]{2,1,0:T(8,128)S(1)}, u32[]{:S(2)}, u32[]{:S(2)}) async-start(f32[128,24,128]{2,1,0:T(8,128)} %scan.1), calls=%async_computation.1 | async-start | bytes 3145728 | tf_op jit(solution)/shard_map/all_to_all | solution.py:259
  75.9 1.2 %copy-start = (f32[128,24,128]{2,1,0:T(8,128)}, f32[128,24,128]{2,1,0:T(8,128)S(1)}, u32[]{:S(2)}) copy-start(f32[128,24,128]{2,1,0:T(8,128)S(1)} %all-to-all-done.1.got) | copy-start | bytes 4718596

commit v2 on v1

--- a/solution.py
+++ b/solution.py
@@ -8,11 +8,19 @@
 HS = 64
 LANES = 128
 TOK = 128
-STATE_ROWS = 8
-ROWS = 24
-PAIRS = 4
+BLOCKS = 8
+STATE_ROWS = HS // BLOCKS
+ROWS_OUT = 18
+ROWS_BACK = 17
+PAIRS = 8
+VMEM = 24 * 2**20
+WRITE = 4
 F32 = jnp.float32
 BF16 = jnp.bfloat16
+
+FULL_ROWS = [slice(n * TOK, (n + 1) * TOK) for n in range(9)]
+FULL_TOK = 9 * TOK
+HALF_ROWS = [slice(n * TOK, (n + 1) * TOK) for n in range(3)]
 
 NN = (((1,), (0,)), ((), ()))
 NT = (((1,), (1,)), ((), ()))
@@ -108,34 +116,44 @@
         bonus = head_sums(g[:, at].astype(F32) * v[:, at].astype(F32), ones)
         bonus = jnp.sum(rp * kp * bonus, axis=0, keepdims=True)
         through = jnp.exp(last) * passes[:1]
-        peers = slice(pair * STATE_ROWS, (pair + 1) * STATE_ROWS)
-        for place, both in ((0, ends), (1, pulls)):
+        rest = cat(through, bonus, axis=0)
+        states = []
+        for both in (ends, pulls):
             both = both[:, :LANES] + both[:, LANES:]
-            state = jnp.where(lane < HS, both[:HS], both[HS:])
-            out[peers, place * STATE_ROWS : (place + 1) * STATE_ROWS] = state.reshape(
-                HS // STATE_ROWS, STATE_ROWS, LANES
-            )
-        rest = cat(through, bonus, jnp.zeros((6, LANES), F32), axis=0)
-        out[peers, 2 * STATE_ROWS :] = jnp.broadcast_to(rest[None], (STATE_ROWS, 8, LANES))
-
-
-def scan_kernel(got, out):
-    shards = got.shape[0]
+            states.append(jnp.where(lane < HS, both[:HS], both[HS:]))
+        for peer in range(BLOCKS):
+            at = (pair * BLOCKS + peer) * ROWS_OUT
+            for place, state in enumerate(states):
+                row = at + place * STATE_ROWS
+                out[row : row + STATE_ROWS] = state[peer * STATE_ROWS : (peer + 1) * STATE_ROWS]
+            out[at + 2 * STATE_ROWS : at + ROWS_OUT] = rest
+
+
+def scan_kernel(got, done, out):
+    del done
+    shards = got.shape[0] // ROWS_OUT
     state = jnp.zeros((STATE_ROWS, LANES), F32)
-    bonus = jnp.zeros((8, LANES), F32)
-    for at in range(shards):
-        out[at, :STATE_ROWS] = state
-        rest = got[at, 2 * STATE_ROWS :]
-        state = rest[:1] * state + got[at, :STATE_ROWS]
-        bonus = bonus + rest
+    bonus = jnp.zeros((1, LANES), F32)
+    for shard in range(shards):
+        at, to = shard * ROWS_OUT, shard * ROWS_BACK
+        out[to : to + STATE_ROWS] = state
+        through = got[at + 2 * STATE_ROWS : at + 2 * STATE_ROWS + 1]
+        state = through * state + got[at : at + STATE_ROWS]
+        bonus = bonus + got[at + 2 * STATE_ROWS + 1 : at + ROWS_OUT]
     state = jnp.zeros((STATE_ROWS, LANES), F32)
-    for at in reversed(range(shards)):
-        out[at, STATE_ROWS : 2 * STATE_ROWS] = state
-        state = got[at, 2 * STATE_ROWS : 2 * STATE_ROWS + 1] * state + got[at, STATE_ROWS : 2 * STATE_ROWS]
-        out[at, 2 * STATE_ROWS :] = bonus
-
-
-def inside_kernel(r, k, v, g, x, cum_in, u, masks, dr, dk, dv, dl):
+    for shard in reversed(range(shards)):
+        at, to = shard * ROWS_OUT, shard * ROWS_BACK
+        out[to + STATE_ROWS : to + 2 * STATE_ROWS] = state
+        out[to + 2 * STATE_ROWS : to + ROWS_BACK] = bonus
+        through = got[at + 2 * STATE_ROWS : at + 2 * STATE_ROWS + 1]
+        state = through * state + got[at + STATE_ROWS : at + 2 * STATE_ROWS]
+
+
+def inside_kernel(r, k, v, g, x, cum_in, u, masks, full_out, half_out, done):
+    done[...] = jnp.zeros(done.shape, F32)
+    dr, dk, dv, dl, rd, kd, pr, pk, rate = (full_out.at[rows] for rows in FULL_ROWS)
+    el, gc, vc = (half_out.at[rows] for rows in HALF_ROWS)
+    through = full_out.at[FULL_TOK:]
     heads = head_masks()
     ones = ones_by_head()
     row, col = square()
@@ -144,13 +162,16 @@
     sums = cat(after, onward, axis=1)
     allowed = cat(masks[0], masks[0], axis=0)
     allowed_t = cat(masks[1], masks[1], axis=0)
+    both = masks[2][TOK - 1 :] * masks[3][TOK - 1 :]
     for pair in range(PAIRS):
         at = slice(pair * LANES, (pair + 1) * LANES)
         rb, kb, vb, gb = r[:, at], k[:, at], v[:, at], g[:, at]
         rp, kp, vp, gp = (part.astype(F32) for part in (rb, kb, vb, gb))
         cum = cum_in[:, at]
-        middle = 0.5 * cum[TOK - 1 :]
-        scale_r = jnp.exp(cum + jnp.exp(x[:, at]) - middle)
+        last = cum[TOK - 1 :]
+        middle = 0.5 * last
+        speed = jnp.exp(x[:, at])
+        scale_r = jnp.exp(cum + speed - middle)
         scale_k = jnp.exp(middle - cum)
         rh, rl = halves(rp * scale_r)
         kh, kl = halves(kp * scale_k)
@@ -172,40 +193,72 @@
         dk[:, at] = dki + own * rp
         high, low = halves(cat(rp * dri, kp * dki, axis=0))
         dl[:, at] = dot(sums, high, NN) + dot(sums, low, NN)
-
-
-def final_kernel(r, k, v, g, x, cum_in, masks, dri, dki, dvi, dli, got, dr, dk, dv, dx, du):
+        reached = jnp.exp(cum + speed) * masks[3]
+        kept = jnp.exp(last - cum) * masks[2]
+        rd[:, at] = reached
+        kd[:, at] = kept
+        pr[:, at] = rp * reached
+        ending = kp * kept
+        pk[:, at] = ending
+        high, low = halves(ending)
+        el[:, at] = low
+        rate[:, at] = speed
+        through[:, at] = jnp.broadcast_to(jnp.exp(last) * both, (8, LANES))
+        gc[:, at] = gb
+        vc[:, at] = vb
+
+
+def final_kernel(full, half, got, dr, dk, dv, dx, du, rounded, sems):
     heads = head_masks()
     row, col = square()
     after = (row < col).astype(F32).astype(BF16)
     earlier = (row > col).astype(F32).astype(BF16)
     sums = cat(after, earlier, axis=1)
-    for pair in range(PAIRS):
+    dri, dki, dvi, dli, rd, kd, pr, pk, rate = (full.at[rows] for rows in FULL_ROWS)
+    el_in, g, v = (half.at[rows] for rows in HALF_ROWS)
+    copies = []
+    for pair in range(du.shape[1] // LANES):
         at = slice(pair * LANES, (pair + 1) * LANES)
-        peers = slice(pair * STATE_ROWS, (pair + 1) * STATE_ROWS)
-        state = got[peers, :STATE_ROWS].reshape(HS, LANES)
-        dstate = got[peers, STATE_ROWS : 2 * STATE_ROWS].reshape(HS, LANES)
-        du[:, at] = got[pair * STATE_ROWS, 2 * STATE_ROWS + 1 : 2 * STATE_ROWS + 2]
-        rp, kp = r[:, at].astype(F32), k[:, at].astype(F32)
-        cum = cum_in[:, at]
-        last = cum[TOK - 1 :]
-        rate = jnp.exp(x[:, at])
-        kd = jnp.exp(last - cum) * masks[2]
-        rd = jnp.exp(cum + rate) * masks[3]
+        rows = [(pair * BLOCKS + peer) * ROWS_BACK for peer in range(BLOCKS)]
+        state = cat(*(got[row : row + STATE_ROWS] for row in rows), axis=0)
+        dstate = cat(*(got[row + STATE_ROWS : row + 2 * STATE_ROWS] for row in rows), axis=0)
+        du[:, at] = got[rows[0] + 2 * STATE_ROWS : rows[0] + ROWS_BACK]
         sh, sl = (by_head(part, heads) for part in halves(state))
         dh, dlow = (by_head(part, heads) for part in halves(dstate))
-        drs = rd * (dot(g[:, at], sh, NN) + dot(g[:, at], sl, NN))
-        dks = kd * (dot(v[:, at], dh, NN) + dot(v[:, at], dlow, NN))
-        eh, el = halves(kp * kd)
-        dvs = dot(eh, dh, NT) + dot(eh, dlow, NT) + dot(el, dh, NT)
-        dr[:, at] = (dri[:, at] + drs).astype(BF16)
-        dk[:, at] = (dki[:, at] + dks).astype(BF16)
-        dv[:, at] = (dvi[:, at] + dvs).astype(BF16)
-        high, low = halves(cat(rp * drs, kp * dks, axis=0))
-        both = masks[2][TOK - 1 :] * masks[3][TOK - 1 :]
-        across = jnp.exp(last) * both * jnp.sum(state * dstate, axis=0, keepdims=True)
-        grad = dli[:, at] + dot(sums, high, NN) + dot(sums, low, NN) + across
-        dx[:, at] = (-rate * grad).astype(BF16)
+        gb, vb = g[:, at], v[:, at]
+        reach = dot(cat(gb, gb, axis=1), cat(sh, sl, axis=0), NN)
+        pull = dot(cat(vb, vb, axis=1), cat(dh, dlow, axis=0), NN)
+        ending = pk[:, at]
+        eh, el = ending.astype(BF16), el_in[:, at]
+        dvs = dot(cat(eh, el, axis=1), cat(dh, dh, axis=1), NT) + dot(eh, dlow, NT)
+        rounded[0, :, at] = (dri[:, at] + rd[:, at] * reach).astype(BF16)
+        rounded[1, :, at] = (dki[:, at] + kd[:, at] * pull).astype(BF16)
+        rounded[2, :, at] = (dvi[:, at] + dvs).astype(BF16)
+        moved = dot(sums, cat(*halves(cat(pr[:, at] * reach, ending * pull, axis=0)), axis=1), NN)
+        across = full[FULL_TOK : FULL_TOK + 1, at] * jnp.sum(state * dstate, axis=0, keepdims=True)
+        grad = dli[:, at] + moved[:, :LANES] + moved[:, LANES:] + across
+        rounded[3, :, at] = (-rate[:, at] * grad).astype(BF16)
+        if (pair + 1) % WRITE == 0:
+            ready = slice((pair + 1 - WRITE) * LANES, (pair + 1) * LANES)
+            for n, out in enumerate((dr, dk, dv, dx)):
+                sem = sems.at[pair // WRITE, n]
+                copies.append(pltpu.make_async_copy(rounded.at[n, :, ready], out.at[:, ready], sem))
+                copies[-1].start()
+    for copy in copies:
+        copy.wait()
+
+
+def hbm(x):
+    return pltpu.with_memory_space_constraint(x, pltpu.HBM)
+
+
+def vm(x):
+    return pltpu.with_memory_space_constraint(x, pltpu.VMEM)
+
+
+def exchange(rows, peers):
+    packets = rows.reshape(peers, -1, 1, LANES)
+    return lax.all_to_all(packets, "seq", 0, 0, tiled=True).reshape(rows.shape)
 
 
 def body(r, k, v, x, u, g, spans):
@@ -214,14 +267,13 @@
     peers = lax.axis_size("seq")
     steps = npairs // PAIRS
     part = PAIRS * LANES
+    r, k, v, x, g, u = (hbm(part) for part in (r, k, v, x, g, u.reshape(1, -1)))
     rank = lax.axis_index("seq").astype(jnp.int32).reshape(1)
     wide = pl.BlockSpec((TOK, part), lambda i, *_: (0, i))
     thin = pl.BlockSpec((1, part), lambda i, *_: (0, i))
-    sent = pl.BlockSpec((PAIRS * STATE_ROWS, ROWS, LANES), lambda i, *_: (i, 0, 0))
+    sent = pl.BlockSpec((PAIRS * BLOCKS * ROWS_OUT, LANES), lambda i, *_: (i, 0))
+    whole = pl.BlockSpec(memory_space=pltpu.VMEM)
     fixed = pl.BlockSpec((4, TOK, LANES), lambda i, *_: (0, 0, 0))
-    full = jax.ShapeDtypeStruct((tokens, width), F32)
-    rounded = jax.ShapeDtypeStruct((tokens, width), BF16)
-    packet = jax.ShapeDtypeStruct((peers, ROWS, LANES), F32)
 
     summaries, cum, masks = pl.pallas_call(
         summary_kernel,
@@ -236,36 +288,56 @@
                 pltpu.VMEM((8, LANES), F32),
             ],
         ),
-        out_shape=[packet, full, jax.ShapeDtypeStruct((4, TOK, LANES), F32)],
+        out_shape=[
+            pltpu.HBM((peers * ROWS_OUT, LANES), F32),
+            pltpu.HBM((tokens, width), F32),
+            pltpu.HBM((4, TOK, LANES), F32),
+        ],
         name="summary",
+        compiler_params=pltpu.CompilerParams(vmem_limit_bytes=VMEM),
         cost_estimate=pl.CostEstimate(flops=10**9, bytes_accessed=6 * 10**6, transcendentals=10**6),
-    )(rank, spans.reshape(1, -1), r, k, v, g, x)
-    got = lax.all_to_all(summaries, "seq", 0, 0, tiled=True)
-    dri, dki, dvi, dli = pl.pallas_call(
+    )(rank, hbm(spans.reshape(1, -1)), r, k, v, g, x)
+    got = exchange(summaries, peers)
+    full, half, done = pl.pallas_call(
         inside_kernel,
         grid=(steps,),
         in_specs=[wide] * 6 + [thin, fixed],
-        out_specs=[wide] * 4,
-        out_shape=[full] * 4,
+        out_specs=[
+            pl.BlockSpec((FULL_TOK + 8, part), lambda i, *_: (0, i)),
+            pl.BlockSpec((3 * TOK, part), lambda i, *_: (0, i)),
+            pl.BlockSpec((8, LANES), lambda i, *_: (0, 0)),
+        ],
+        out_shape=[
+            pltpu.HBM((FULL_TOK + 8, width), F32),
+            pltpu.HBM((3 * TOK, width), BF16),
+            pltpu.HBM((8, LANES), F32),
+        ],
         name="inside",
+        compiler_params=pltpu.CompilerParams(vmem_limit_bytes=VMEM),
         cost_estimate=pl.CostEstimate(flops=10**10, bytes_accessed=10**7, transcendentals=10**6),
-    )(r, k, v, g, x, cum, u.reshape(1, -1), masks)
+    )(r, k, v, g, x, hbm(cum), u, hbm(masks))
     states = pl.pallas_call(
         scan_kernel,
-        out_shape=packet,
+        in_specs=[whole, pl.BlockSpec(memory_space=pl.ANY)],
+        out_shape=pltpu.VMEM((peers * ROWS_BACK, LANES), F32),
         name="scan",
-        cost_estimate=pl.CostEstimate(flops=10**6, bytes_accessed=3 * 10**6, transcendentals=0),
-    )(got)
-    returned = lax.all_to_all(states, "seq", 0, 0, tiled=True)
+        compiler_params=pltpu.CompilerParams(vmem_limit_bytes=VMEM),
+        cost_estimate=pl.CostEstimate(flops=10**10, bytes_accessed=3 * 10**7, transcendentals=0),
+    )(vm(got), hbm(done))
+    returned = exchange(states, peers)
     dr, dk, dv, dx, du = pl.pallas_call(
         final_kernel,
-        grid=(steps,),
-        in_specs=[wide] * 6 + [fixed] + [wide] * 4 + [sent],
-        out_specs=[wide] * 4 + [thin],
-        out_shape=[rounded] * 4 + [jax.ShapeDtypeStruct((1, width), F32)],
+        in_specs=[whole] * 3,
+        out_specs=[pl.BlockSpec(memory_space=pl.ANY)] * 4 + [whole],
+        out_shape=[pltpu.HBM((tokens, width), BF16)] * 4 + [jax.ShapeDtypeStruct((1, width), F32)],
+        scratch_shapes=[
+            pltpu.VMEM((4, tokens, width), BF16),
+            pltpu.SemaphoreType.DMA((npairs // WRITE, 4)),
+        ],
         name="final",
+        compiler_params=pltpu.CompilerParams(vmem_limit_bytes=VMEM),
         cost_estimate=pl.CostEstimate(flops=10**9, bytes_accessed=10**7, transcendentals=10**6),
-    )(r, k, v, g, x, cum, masks, dri, dki, dvi, dli, returned)
+    )(vm(full), vm(half), vm(returned))
     return dr, dk, dv, dx, du.reshape(width)
 
 

time: 85.5 us -> 68.4 us (0.80)
  blocking collectives: 36.2 us -> 24.3 us
  starting transfers between devices: 4.69 us -> 11.5 us
  waiting for transfers between devices: 10.7 us -> 4.97 us
  Pallas kernels: 31.7 us -> 26.8 us
  local copies, waits for them, and re-layouts: 1.15 us -> 0.01 us
    all_to_all x1, blocking collectives: 36.2 us -> 24.3 us  [exchange(): return lax.all_to_all(packets, 'seq', 0, 0, tiled=True).reshape(rows.shape)]
    all_to_all x1, starting transfers between devices: 4.69 us -> 11.5 us  [exchange(): return lax.all_to_all(packets, 'seq', 0, 0, tiled=True).reshape(rows.shape)]
    pallas_call x2, Pallas kernels: 10.9 us -> 5.08 us  [the longest x1 4.76 us: body(): pl.pallas_call(final_kernel, in_specs=[whole] * 3, out_specs=[pl.BlockSpe...]
    all_to_all x1, waiting for transfers between devices: 10.7 us -> 4.97 us  [exchange(): return lax.all_to_all(packets, 'seq', 0, 0, tiled=True).reshape(rows.shape)]
    pallas_call x1, Pallas kernels: 14 us -> 15.4 us  [body(): pl.pallas_call(inside_kernel, grid=(steps,), in_specs=[wide] * 6 + [thin,...]
    unnamed x2 -> x8, local copies, waits for them, and re-layouts: 1.15 us -> 0.01 us
  transfers between devices with their start and end apart: 1 -> 1, of which waited for: 1 -> 1; matrix products, arithmetic and copies ran while one was open for 0% -> 0% of each run, Pallas kernels for 16% -> 23%
where the time goes in v2:
time: 68.4 us; the launch traced here: 68.2 us
  Pallas kernels  26.8 us (39%)
  blocking collectives  24.3 us (36%)
  starting transfers between devices  11.5 us (17%)
  waiting for transfers between devices  4.97 us (7%)
    all_to_all x1, blocking collectives, exchange(): return lax.all_to_all(packets, 'seq', 0, 0, tiled=True).reshape(rows.shape)  24.3 us
    pallas_call x1, Pallas kernels, body(): pl.pallas_call(inside_kernel, grid=(steps,), in_specs=[wide] * 6 + [thin,...  15.4 us
    all_to_all x1, starting transfers between devices, exchange(): return lax.all_to_all(packets, 'seq', 0, 0, tiled=True).reshape(rows.shape)  11.5 us
    pallas_call x1, Pallas kernels, body(): pl.pallas_call(summary_kernel, grid_spec=pltpu.PrefetchScalarGridSpec(num...  6.31 us
    all_to_all x1, waiting for transfers between devices, exchange(): return lax.all_to_all(packets, 'seq', 0, 0, tiled=True).reshape(rows.shape)  4.97 us
    pallas_call x1, Pallas kernels, body(): pl.pallas_call(final_kernel, in_specs=[whole] * 3, out_specs=[pl.BlockSpe...  4.76 us
  transfers between devices with their start and end apart: 1, of which 1 were waited for; matrix products, arithmetic and copies ran while one was open for 0% of the time, Pallas kernels for 23%

profile of v2, /device:TPU:1, one launch (start us, length us, event | category | flops | bytes accessed | tf_op | source)
XLA Modules:
  0.0 68.2 jit_solution(11010867382124679992)
XLA Ops:
  0.6 6.3 %summary.1 = (f32[2304,128]{1,0:T(8,128)}, f32[128,2048]{1,0:T(8,128)}, f32[4,128,128]{2,1,0:T(8,128)}) custom-call(s32[1]{0:T(128)} %bitcast.rank, s32[1,256]{1,0:T(1,128)} %bitcast.16, bf16[128,2048]{1,0:T(8,128)(2,1)} %r.3, bf16[128,2048]{1,0:T(8,128)(2,1)} %k.3, bf16[128,2048]{1,0:T(8,128)(2,1)} %v.3, bf16[128,2048]{1,0:T(8,128)(2,1)} %g.3, f32[128,2048]{1,0:T(8,128)} %x.3), custom_call_target="tpu_custom_call" | custom-call | flops 1000000000 | bytes 6000000 | tf_op jit(solution)/shard_map/summary/pallas_call | solution.py:278
  6.9 11.5 %all-to-all-start = ((f32[128,18,1,128]{3,2,1,0:T(1,128)}), f32[128,18,1,128]{3,2,1,0:T(1,128)S(1)}, u32[]{:S(2)}, u32[]{:S(2)}) async-start(f32[128,18,1,128]{3,2,1,0:T(1,128)} %bitcast.13), calls=%async_computation | async-start | bytes 2359296 | tf_op jit(solution)/shard_map/all_to_all | solution.py:261
  18.4 15.4 %inside.1 = (f32[1160,2048]{1,0:T(8,128)}, bf16[384,2048]{1,0:T(8,128)(2,1)}, f32[8,128]{1,0:T(8,128)}) custom-call(bf16[128,2048]{1,0:T(8,128)(2,1)} %r.3, bf16[128,2048]{1,0:T(8,128)(2,1)} %k.3, bf16[128,2048]{1,0:T(8,128)(2,1)} %v.3, bf16[128,2048]{1,0:T(8,128)(2,1)} %g.3, f32[128,2048]{1,0:T(8,128)} %x.3, f32[128,2048]{1,0:T(8,128)} %get-tuple-element.16.cum_in, ...), custom_call_target="tpu_custom_call" | custom-call | flops 10000000000 | bytes 10000000 | tf_op jit(solution)/shard_map/inside/pallas_call | solution.py:301
  33.8 5.0 %all-to-all-done = f32[128,18,1,128]{3,2,1,0:T(1,128)S(1)} async-done(((f32[128,18,1,128]{3,2,1,0:T(1,128)}), f32[128,18,1,128]{3,2,1,0:T(1,128)S(1)}, u32[]{:S(2)}, u32[]{:S(2)}) %all-to-all-start) | async-done | bytes 1179680 | tf_op jit(solution)/shard_map/all_to_all | solution.py:261
  38.8 0.0 slice-start
  38.8 0.0 slice-start.1
  38.8 0.0 slice-start.2
  38.8 0.3 scan.1
  39.1 0.0 copy-start
  39.1 24.3 %all_to_all.10 = f32[128,17,1,128]{3,2,1,0:T(1,128)S(1)} all-to-all(f32[128,17,1,128]{3,2,1,0:T(1,128)S(1)} %bitcast.12), channel_id=1, replica_groups=mesh['seq'=128] {'seq'}, dimensions={0} | all-to-all | bytes 2228224 | tf_op jit(solution)/shard_map/all_to_all | solution.py:261
  63.4 0.0 slice-done
  63.4 0.0 slice-done.1
  63.4 0.0 slice-done.2
  63.4 0.0 copy-done
  63.4 4.8 %final.1 = (bf16[128,2048]{1,0:T(8,128)(2,1)}, bf16[128,2048]{1,0:T(8,128)(2,1)}, bf16[128,2048]{1,0:T(8,128)(2,1)}, bf16[128,2048]{1,0:T(8,128)(2,1)}, f32[1,2048]{1,0:T(1,128)}) custom-call(f32[1160,2048]{1,0:T(8,128)S(1)} %bitcast.9, bf16[384,2048]{1,0:T(8,128)(2,1)S(1)} %copy-done, f32[2176,128]{1,0:T(8,128)S(1)} %bitcast.10), custom_call_target="tpu_custom_call" | custom-call | flops 1000000000 | bytes 10000000 | tf_op jit(solution)/shard_map/final/pallas_call | solution.py:328
  (1 shorter events, 0.0 us)
Async XLA Ops:
  6.9 31.8 %all-to-all-start = ((f32[128,18,1,128]{3,2,1,0:T(1,128)}), f32[128,18,1,128]{3,2,1,0:T(1,128)S(1)}, u32[]{:S(2)}, u32[]{:S(2)}) async-start(f32[128,18,1,128]{3,2,1,0:T(1,128)} %bitcast.13), calls=%async_computation | async-start | bytes 2359296 | tf_op jit(solution)/shard_map/all_to_all | solution.py:261
  38.8 24.6 %slice-start = ((s8[9502720]{0:T(1024)(128)(4,1)}), s8[4194304]{0:T(1024)(128)(4,1)S(1)}, s32[]{:S(2)}) async-start(s8[9502720]{0:T(1024)(128)(4,1)} %bitcast.8), calls=%async_computation.2 | async-start | bytes 8388608
  38.8 24.6 %slice-start.1 = ((s8[9502720]{0:T(1024)(128)(4,1)}), s8[4194304]{0:T(1024)(128)(4,1)S(1)}, s32[]{:S(2)}) async-start(s8[9502720]{0:T(1024)(128)(4,1)} %bitcast.8), calls=%async_computation.3 | async-start | bytes 8388608
  38.8 24.6 %slice-start.2 = ((s8[9502720]{0:T(1024)(128)(4,1)}), s8[1114112]{0:T(1024)(128)(4,1)S(1)}, s32[]{:S(2)}) async-start(s8[9502720]{0:T(1024)(128)(4,1)} %bitcast.8), calls=%async_computation.4 | async-start | bytes 2228224
  39.1 24.3 %copy-start = (bf16[384,2048]{1,0:T(8,128)(2,1)S(1)}, bf16[384,2048]{1,0:T(8,128)(2,1)}, u32[]{:S(2)}) copy-start(bf16[384,2048]{1,0:T(8,128)(2,1)} %get-tuple-element.19.half) | copy-start | bytes 4718596

commit v3 on v2

v3 whole, which is shorter than its diff:
```python
import jax
import jax.numpy as jnp
from jax import lax
from jax.experimental import pallas as pl
from jax.experimental.pallas import tpu as pltpu
from jax.sharding import Mesh
from jax.sharding import PartitionSpec as P

HS = 64
LANES = 128
TOK = 128
CORES = 2
HALF = 8
BLOCKS = 8
STATE_ROWS = HS // BLOCKS
ROWS_OUT = 18
ROWS_BACK = 17
PULL = HALF * HS
DECAY = 2 * PULL
BONUS = DECAY + HALF
GROUP = 4
INSIDE = 4
PAIRS = 8
VMEM = 24 * 2**20
WRITE = 4
LOG2_E = 1.4426950408889634
LOG2_LOG2_E = 0.5287663729448977
LN_2 = 0.6931471805599453
F32 = jnp.float32
BF16 = jnp.bfloat16

FULL_ROWS = [slice(n * TOK, (n + 1) * TOK) for n in range(9)]
FULL_TOK = 9 * TOK
HALF_ROWS = [slice(n * TOK, (n + 1) * TOK) for n in range(3)]

NN = (((1,), (0,)), ((), ()))
NT = (((1,), (1,)), ((), ()))
TN = (((0,), (0,)), ((), ()))


def dot(a, b, dims):
    return lax.dot_general(a, b, dims, preferred_element_type=F32)


def halves(x):
    high = x.astype(BF16)
    return high, (x - high.astype(F32)).astype(BF16)


def head_masks():
    lane = lax.broadcasted_iota(jnp.int32, (1, LANES), 1)
    return (lane < HS).astype(F32).astype(BF16), (lane >= HS).astype(F32).astype(BF16)


def by_head(x, masks):
    return jnp.concatenate([x * masks[0], x * masks[1]], axis=0)


def side_by_side(x):
    return jnp.concatenate([x[:TOK], x[TOK:]], axis=1)


def cat(*parts, axis):
    return jnp.concatenate(parts, axis=axis)


def square(n=TOK):
    row = lax.broadcasted_iota(jnp.int32, (n, n), 0)
    return row, lax.broadcasted_iota(jnp.int32, (n, n), 1)


def ones_by_head():
    row, col = square()
    same = ((row < HS) == (col < HS)).astype(F32).astype(BF16)
    return cat(same, same, axis=0)


def head_sums(x, ones):
    high, low = halves(x)
    return dot(cat(high, low, axis=1), ones, NN)


def segments(spans, base):
    ndocs = spans.shape[1]
    row, col = square(ndocs)
    upper = (row <= col).astype(F32).astype(BF16)
    spans = jnp.broadcast_to(spans, (8, ndocs))
    coarse, fine = ((part.astype(F32)).astype(BF16) for part in (spans >> 6, spans & 63))
    ends = (64.0 * dot(coarse, upper, NN) + dot(fine, upper, NN))[:1]
    down = (base + lax.broadcasted_iota(jnp.int32, (TOK, 1), 0)).astype(F32)
    seg_down = jnp.sum(jnp.where(ends <= down, 1.0, 0.0), axis=1, keepdims=True)
    row, col = square()
    seg_across = jnp.sum(jnp.where(row == col, seg_down, 0.0), axis=0, keepdims=True)
    prev = jnp.sum(jnp.where(ends <= down[:1] - 1.0, 1.0, 0.0), axis=1, keepdims=True)
    return seg_across, seg_down, jnp.where(down[:1] > 0.0, prev, -1.0)


def decay_rate(x):
    return jnp.exp2(x * LOG2_E + LOG2_LOG2_E)


def summary_kernel(spans, r, k, v, g, x, out, cum_out, masks_out, keep, carried, passes):
    @pl.when(pl.program_id(0) == 0)
    def _():
        seg_across, seg_down, prev = segments(spans[...], (lax.axis_index("chip") * CORES + lax.axis_index("core")) * TOK)
        row, col = square()
        same = seg_down == seg_across
        last = seg_down[TOK - 1 :]
        keep[...] = jnp.broadcast_to((seg_down == last).astype(F32), (TOK, LANES))
        carried[...] = jnp.broadcast_to((seg_down == prev).astype(F32), (TOK, LANES))
        passes[...] = jnp.broadcast_to((last == prev).astype(F32), passes.shape)
        masks_out[0] = (same & (row > col)).astype(F32)
        masks_out[1] = (same & (row < col)).astype(F32)
        masks_out[2] = keep[...]
        masks_out[3] = carried[...]

    row, col = square()
    lower = (row >= col).astype(F32).astype(BF16)
    lower = cat(lower, lower, axis=1)
    ones = ones_by_head()
    lane = lax.broadcasted_iota(jnp.int32, (HS, LANES), 1)
    spots = [slice(pair * LANES, (pair + 1) * LANES) for pair in range(PAIRS)]
    for group in range(0, PAIRS, GROUP):
        wide = slice(group * LANES, (group + GROUP) * LANES)
        cum_out[:, wide] = dot(lower, cat(*halves(decay_rate(x[:, wide])), axis=0), NN)
    products = [cat(*halves(g[:, at].astype(F32) * v[:, at].astype(F32)), axis=1) for at in spots]
    bonuses = dot(cat(*products, axis=0), ones, NN)
    endings, reaches = [], []
    for at in spots:
        cum = cum_out[:, at]
        rp, kp = r[:, at].astype(F32), k[:, at].astype(F32)
        ending = kp * jnp.exp2(cum - cum[TOK - 1 :]) * keep[...]
        reached = rp * jnp.exp2(decay_rate(x[:, at]) - cum) * carried[...]
        endings.append(cat(*halves(ending), axis=1))
        reaches.append(cat(*halves(reached), axis=1))
    ends = [dot(v[:, at], ending, TN) for at, ending in zip(spots, endings)]
    pulls = [dot(g[:, at], reached, TN) for at, reached in zip(spots, reaches)]
    for pair, at in enumerate(spots):
        for place, both in ((0, ends[pair]), (PULL, pulls[pair])):
            both = both[:, :LANES] + both[:, LANES:]
            state = jnp.where(lane < HS, both[:HS], both[HS:])
            out[0, place + pair * HS : place + (pair + 1) * HS] = state
        bonus = r[:, at].astype(F32) * k[:, at].astype(F32) * bonuses[pair * TOK : (pair + 1) * TOK]
        through = jnp.exp2(-cum_out[TOK - 1 :, at]) * passes[:1]
        out[0, DECAY + pair : DECAY + pair + 1] = through
        out[0, BONUS + pair : BONUS + pair + 1] = jnp.sum(bonus, axis=0, keepdims=True)


def combine_kernel(got, out, done):
    done[...] = jnp.zeros(done.shape, F32)
    first, second = got.at[0], got.at[1]
    for pair in range(HALF):
        rows = slice(pair * HS, (pair + 1) * HS)
        below = slice(PULL + pair * HS, PULL + (pair + 1) * HS)
        near = first[DECAY + pair : DECAY + pair + 1]
        far = second[DECAY + pair : DECAY + pair + 1]
        ends = far * first[rows] + second[rows]
        pulls = first[below] + near * second[below]
        bonus = first[BONUS + pair : BONUS + pair + 1] + second[BONUS + pair : BONUS + pair + 1]
        rest = cat(near * far, bonus, axis=0)
        for peer in range(BLOCKS):
            at = (pair * BLOCKS + peer) * ROWS_OUT
            for place, state in enumerate((ends, pulls)):
                row = at + place * STATE_ROWS
                out[row : row + STATE_ROWS] = state[peer * STATE_ROWS : (peer + 1) * STATE_ROWS]
            out[at + 2 * STATE_ROWS : at + ROWS_OUT] = rest


def expand_kernel(got, sums, before, out):
    del before
    first, second = sums.at[0], sums.at[1]
    for pair in range(HALF):
        rows = slice(pair * HS, (pair + 1) * HS)
        below = slice(PULL + pair * HS, PULL + (pair + 1) * HS)
        starts = [(pair * BLOCKS + peer) * ROWS_BACK for peer in range(BLOCKS)]
        state = cat(*(got[row : row + STATE_ROWS] for row in starts), axis=0)
        dstate = cat(*(got[row + STATE_ROWS : row + 2 * STATE_ROWS] for row in starts), axis=0)
        bonus = got[starts[0] + 2 * STATE_ROWS : starts[0] + ROWS_BACK]
        near = first[DECAY + pair : DECAY + pair + 1]
        far = second[DECAY + pair : DECAY + pair + 1]
        out[0, rows] = state
        out[0, below] = far * dstate + second[below]
        out[1, rows] = near * state + first[rows]
        out[1, below] = dstate
        for core in range(CORES):
            out[core, DECAY + pair : DECAY + pair + 1] = bonus


def scan_kernel(got, before, out, done):
    del before
    done[...] = jnp.zeros(done.shape, F32)
    shards = got.shape[0] // ROWS_OUT
    state = jnp.zeros((STATE_ROWS, LANES), F32)
    bonus = jnp.zeros((1, LANES), F32)
    for shard in range(shards):
        at, to = shard * ROWS_OUT, shard * ROWS_BACK
        out[to : to + STATE_ROWS] = state
        through = got[at + 2 * STATE_ROWS : at + 2 * STATE_ROWS + 1]
        state = through * state + got[at : at + STATE_ROWS]
        bonus = bonus + got[at + 2 * STATE_ROWS + 1 : at + ROWS_OUT]
    state = jnp.zeros((STATE_ROWS, LANES), F32)
    for shard in reversed(range(shards)):
        at, to = shard * ROWS_OUT, shard * ROWS_BACK
        out[to + STATE_ROWS : to + 2 * STATE_ROWS] = state
        out[to + 2 * STATE_ROWS : to + ROWS_BACK] = bonus
        through = got[at + 2 * STATE_ROWS : at + 2 * STATE_ROWS + 1]
        state = through * state + got[at + STATE_ROWS : at + 2 * STATE_ROWS]


def inside_kernel(r, k, v, g, x, cum_in, u, masks, combined, full_out, half_out, done):
    del combined
    done[...] = jnp.zeros(done.shape, F32)
    dr, dk, dv, dl, rd, kd, pr, pk, rate = (full_out.at[rows] for rows in FULL_ROWS)
    el, gc, vc = (half_out.at[rows] for rows in HALF_ROWS)
    through = full_out.at[FULL_TOK:]
    heads = head_masks()
    ones = ones_by_head()
    row, col = square()
    after = (row < col).astype(F32).astype(BF16)
    onward = -((row <= col).astype(F32).astype(BF16))
    sums = cat(after, onward, axis=1)
    allowed = cat(masks[0], masks[0], axis=1)
    later = cat(masks[1], masks[1], axis=1) > 0.0
    both = masks[2][TOK - 1 :] * masks[3][TOK - 1 :]
    spots = [slice(pair * LANES, (pair + 1) * LANES) for pair in range(r.shape[1] // LANES)]
    scaled, products = [], []
    for at in spots:
        rp, kp, vp, gp = (part[:, at].astype(F32) for part in (r, k, v, g))
        cum = cum_in[:, at]
        last = cum[TOK - 1 :]
        middle = 0.5 * last
        speed = decay_rate(x[:, at])
        scale_r = jnp.exp2(middle + (speed - cum))
        scale_k = jnp.exp2(cum - middle)
        scaled.append((scale_r, scale_k, halves(rp * scale_r), halves(kp * scale_k)))
        products += [cat(*halves(rp * u[:, at] * kp), axis=1), cat(*halves(gp * vp), axis=1)]
        reached = jnp.exp2(speed - cum) * masks[3]
        kept = jnp.exp2(cum - last) * masks[2]
        rd[:, at] = reached
        kd[:, at] = kept
        pr[:, at] = rp * reached
        ending = kp * kept
        pk[:, at] = ending
        el[:, at] = halves(ending)[1]
        rate[:, at] = -LN_2 * speed
        through[:, at] = jnp.broadcast_to(jnp.exp2(-last) * both, (8, LANES))
        gc[:, at] = g[:, at]
        vc[:, at] = v[:, at]
    own = dot(cat(*products, axis=0), ones, NN)
    pulls, scores = [], []
    for at, (_, _, (rh, rl), (kh, kl)) in zip(spots, scaled):
        g2 = by_head(g[:, at], heads)
        pulls.append(halves(side_by_side(dot(g2, v[:, at], NT)) * allowed))
        score = dot(cat(by_head(kh, heads), by_head(kl, heads), axis=1), cat(rh, rh, axis=1), NT)
        score = score + dot(by_head(kh, heads), rl, NT)
        scores.append(halves(jnp.where(later, side_by_side(score), 0.0)))
    flipped = [[cat(part[:, :TOK].T, part[:, TOK:].T, axis=1) for part in pull] for pull in pulls]
    paired = []
    for pair, at in enumerate(spots):
        scale_r, scale_k, (rh, rl), (kh, kl) = scaled[pair]
        rh2, rl2, kh2, kl2 = (by_head(part, heads) for part in (rh, rl, kh, kl))
        (ph, plow), (th, tl), (sh, sl) = pulls[pair], flipped[pair], scores[pair]
        g2 = by_head(g[:, at], heads)
        rp, kp, gp = (part[:, at].astype(F32) for part in (r, k, g))
        mine = own[2 * pair * TOK : (2 * pair + 1) * TOK]
        dot_gv = u[:, at] * own[(2 * pair + 1) * TOK : (2 * pair + 2) * TOK]
        dv[:, at] = dot(sh, g2, NN) + dot(sl, g2, NN) + mine * gp
        dri = scale_r * (dot(ph, kh2, NN) + dot(ph, kl2, NN) + dot(plow, kh2, NN))
        dki = scale_k * (dot(th, rh2, NN) + dot(th, rl2, NN) + dot(tl, rh2, NN))
        dr[:, at] = dri + dot_gv * kp
        dk[:, at] = dki + dot_gv * rp
        paired.append(cat(*halves(cat(rp * dri, kp * dki, axis=0)), axis=1))
    moved = [dot(sums, part, NN) for part in paired]
    for at, part in zip(spots, moved):
        dl[:, at] = part[:, :LANES] + part[:, LANES:]


def final_kernel(full_a, narrow_a, full_b, narrow_b, got, dr, dk, dv, dx, du, rounded, sems):
    heads = head_masks()
    row, col = square()
    after = (row < col).astype(F32).astype(BF16)
    earlier = (row > col).astype(F32).astype(BF16)
    sums = cat(after, earlier, axis=1)
    copies = []
    for base in range(0, du.shape[1] // LANES, WRITE):
        half = base // HALF
        full, narrow = ((full_a, narrow_a), (full_b, narrow_b))[half]
        dri, dki, dvi, dli, rd, kd, pr, pk, rate = (full.at[rows] for rows in FULL_ROWS)
        el_in, g, v = (narrow.at[rows] for rows in HALF_ROWS)
        places = range(base % HALF, base % HALF + WRITE)
        spots = [slice(place * LANES, (place + 1) * LANES) for place in places]
        targets = [slice(pair * LANES, (pair + 1) * LANES) for pair in range(base, base + WRITE)]
        loaded, across = [], []
        for place, at, to in zip(places, spots, targets):
            state = got[half, place * HS : (place + 1) * HS]
            dstate = got[half, PULL + place * HS : PULL + (place + 1) * HS]
            du[:, to] = got[half, DECAY + place : DECAY + place + 1]
            loaded.append([by_head(part, heads) for part in halves(state) + halves(dstate)])
            across.append(full[FULL_TOK : FULL_TOK + 1, at] * jnp.sum(state * dstate, axis=0, keepdims=True))
        reaches, pulls, values = [], [], []
        for at, (sh, sl, dh, dlow) in zip(spots, loaded):
            gb, vb = g[:, at], v[:, at]
            reaches.append(dot(cat(gb, gb, axis=1), cat(sh, sl, axis=0), NN))
            pulls.append(dot(cat(vb, vb, axis=1), cat(dh, dlow, axis=0), NN))
            eh, el = pk[:, at].astype(BF16), el_in[:, at]
            values.append(dot(cat(eh, el, axis=1), cat(dh, dh, axis=1), NT) + dot(eh, dlow, NT))
        paired = []
        for at, reach, pull in zip(spots, reaches, pulls):
            paired.append(cat(*halves(cat(pr[:, at] * reach, pk[:, at] * pull, axis=0)), axis=1))
        moved = [dot(sums, part, NN) for part in paired]
        for n, (at, to) in enumerate(zip(spots, targets)):
            rounded[0, :, to] = (dri[:, at] + rd[:, at] * reaches[n]).astype(BF16)
            rounded[1, :, to] = (dki[:, at] + kd[:, at] * pulls[n]).astype(BF16)
            rounded[2, :, to] = (dvi[:, at] + values[n]).astype(BF16)
            grad = dli[:, at] + moved[n][:, :LANES] + moved[n][:, LANES:] + across[n]
            rounded[3, :, to] = (rate[:, at] * grad).astype(BF16)
        ready = slice(base * LANES, (base + WRITE) * LANES)
        for n, out in enumerate((dr, dk, dv, dx)):
            copies.append(pltpu.make_async_copy(rounded.at[n, :, ready], out.at[:, ready], sems.at[base // WRITE, n]))
            copies[-1].start()
    for copy in copies:
        copy.wait()


def hbm(x):
    return pltpu.with_memory_space_constraint(x, pltpu.HBM)


def vm(x):
    return pltpu.with_memory_space_constraint(x, pltpu.VMEM)


def exchange(rows, peers, axis):
    packets = rows.reshape(peers, -1, 1, LANES)
    return lax.all_to_all(packets, axis, 0, 0, tiled=True).reshape(rows.shape)


def body(r, k, v, x, u, g, spans):
    tokens, width = r.shape
    npairs = width // LANES
    chips = lax.axis_size("chip")
    steps = npairs // PAIRS
    part = PAIRS * LANES
    r, k, v, x, g, u = (hbm(part) for part in (r, k, v, x, g, u.reshape(1, -1)))
    wide = pl.BlockSpec((TOK, part), lambda i: (0, i))
    thin = pl.BlockSpec((1, part), lambda i: (0, i))
    fixed = pl.BlockSpec((4, TOK, LANES), lambda i: (0, 0, 0))
    whole = pl.BlockSpec(memory_space=pltpu.VMEM)
    token = pl.BlockSpec(memory_space=pl.ANY)
    params = pltpu.CompilerParams(vmem_limit_bytes=VMEM)
    assert PAIRS == HALF

    def cost(flops, moved):
        return pl.CostEstimate(flops=flops, bytes_accessed=moved, transcendentals=0)

    def inside(half, after):
        part = INSIDE * LANES
        here = half * HALF // INSIDE
        wide = pl.BlockSpec((TOK, part), lambda i: (0, i + here))
        return pl.pallas_call(
            inside_kernel,
            grid=(HALF // INSIDE,),
            in_specs=[wide] * 6 + [pl.BlockSpec((1, part), lambda i: (0, i + here)), fixed, token],
            out_specs=[
                pl.BlockSpec((FULL_TOK + 8, part), lambda i: (0, i)),
                pl.BlockSpec((3 * TOK, part), lambda i: (0, i)),
                pl.BlockSpec((8, LANES), lambda i: (0, 0)),
            ],
            out_shape=[
                pltpu.HBM((FULL_TOK + 8, HALF * LANES), F32),
                pltpu.HBM((3 * TOK, HALF * LANES), BF16),
                pltpu.HBM((8, LANES), F32),
            ],
            name="inside",
            compiler_params=params,
            cost_estimate=cost(10**10, 10**7),
        )(r, k, v, g, x, hbm(cum), u, hbm(masks), hbm(after))

    summaries, cum, masks = pl.pallas_call(
        summary_kernel,
        grid=(steps,),
        in_specs=[pl.BlockSpec((1, spans.shape[0]), lambda i: (0, 0))] + [wide] * 5,
        out_specs=[pl.BlockSpec((1, BONUS + HALF, LANES), lambda i: (i, 0, 0)), wide, fixed],
        scratch_shapes=[
            pltpu.VMEM((TOK, LANES), F32),
            pltpu.VMEM((TOK, LANES), F32),
            pltpu.VMEM((8, LANES), F32),
        ],
        out_shape=[
            jax.ShapeDtypeStruct((CORES, BONUS + HALF, LANES), F32),
            pltpu.HBM((tokens, width), F32),
            pltpu.HBM((4, TOK, LANES), F32),
        ],
        name="summary",
        compiler_params=params,
        cost_estimate=cost(10**9, 6 * 10**6),
    )(hbm(spans.reshape(1, -1)), r, k, v, g, x)
    both = lax.all_to_all(summaries, "core", 0, 0, tiled=True)
    packets, combined = pl.pallas_call(
        combine_kernel,
        in_specs=[whole],
        out_specs=[whole, whole],
        out_shape=[jax.ShapeDtypeStruct((chips * ROWS_OUT, LANES), F32), pltpu.HBM((8, LANES), F32)],
        name="combine",
        compiler_params=params,
        cost_estimate=cost(10**6, 2 * 10**6),
    )(both)
    got = exchange(packets, chips, "chip")
    first, narrow_first, done = inside(0, combined)
    states, scanned = pl.pallas_call(
        scan_kernel,
        in_specs=[whole, token],
        out_specs=[whole, whole],
        out_shape=[jax.ShapeDtypeStruct((chips * ROWS_BACK, LANES), F32), pltpu.HBM((8, LANES), F32)],
        name="scan",
        compiler_params=params,
        cost_estimate=cost(10**10, 3 * 10**7),
    )(vm(got), hbm(done))
    returned = exchange(states, chips, "chip")
    second, narrow_second, done = inside(1, scanned)
    starts = pl.pallas_call(
        expand_kernel,
        in_specs=[whole, whole, token],
        out_specs=whole,
        out_shape=jax.ShapeDtypeStruct((CORES, BONUS, LANES), F32),
        name="expand",
        compiler_params=params,
        cost_estimate=cost(10**10, 3 * 10**7),
    )(returned, both, hbm(done))
    starts = lax.all_to_all(starts, "core", 0, 0, tiled=True)
    dr, dk, dv, dx, du = pl.pallas_call(
        final_kernel,
        in_specs=[whole] * 5,
        out_specs=[pl.BlockSpec(memory_space=pl.ANY)] * 4 + [whole],
        out_shape=[pltpu.HBM((tokens, width), BF16)] * 4 + [jax.ShapeDtypeStruct((1, width), F32)],
        scratch_shapes=[
            pltpu.VMEM((4, tokens, width), BF16),
            pltpu.SemaphoreType.DMA((npairs // WRITE, 4)),
        ],
        name="final",
        compiler_params=params,
        cost_estimate=cost(10**9, 10**7),
    )(vm(first), vm(narrow_first), vm(second), vm(narrow_second), vm(starts))
    return dr, dk, dv, dx, du.reshape(width)


def solution(mesh):
    chips = Mesh(mesh.devices.reshape(-1, CORES), ("chip", "core"))
    split, whole = P(("chip", "core"), None), P()
    return jax.shard_map(
        body,
        mesh=chips,
        in_specs=(split, split, split, split, whole, split, whole),
        out_specs=(split, split, split, split, whole),
        check_vma=False,
    )
```

time: 68.4 us -> 64.2 us (0.939)
  blocking collectives: 24.3 us -> 13.5 us
  waiting for transfers between devices: 4.97 us -> 11.5 us
  Pallas kernels: 26.8 us -> 21.8 us
  starting transfers between devices: 11.5 us -> 16.3 us
    all_to_all x1 -> x2, blocking collectives: 24.3 us -> 13.5 us  [the longest x1 7.94 us: body(): starts = lax.all_to_all(starts, 'core', 0, 0, tiled=True)]
    all_to_all x1 -> x2, waiting for transfers between devices: 4.97 us -> 11.5 us  [exchange(): return lax.all_to_all(packets, axis, 0, 0, tiled=True).reshape(rows.shape)]
    pallas_call x4 -> x7, Pallas kernels: 26.8 us -> 21.8 us  [the longest x2 12.3 us: inside(): pl.pallas_call(inside_kernel, grid=(HALF // INSIDE,), in_specs=[wide] * 6...]
    all_to_all x1 -> x2, starting transfers between devices: 11.5 us -> 16.3 us  [exchange(): return lax.all_to_all(packets, axis, 0, 0, tiled=True).reshape(rows.shape)]
  transfers between devices with their start and end apart: 1 -> 2, of which waited for: 1 -> 2; matrix products, arithmetic and copies ran while one was open for 0% -> 0% of each run, Pallas kernels for 23% -> 19%
where the time goes in v3:
time: 64.2 us; the launch traced here: 63.8 us
  Pallas kernels  21.8 us (34%)
  starting transfers between devices  16.3 us (25%)
  blocking collectives  13.5 us (21%)
  waiting for transfers between devices  11.5 us (18%)
  between operations  0.72 us (1%)
    all_to_all x2, starting transfers between devices, exchange(): return lax.all_to_all(packets, axis, 0, 0, tiled=True).reshape(rows.shape)  16.3 us
    pallas_call x2, Pallas kernels, inside(): pl.pallas_call(inside_kernel, grid=(HALF // INSIDE,), in_specs=[wide] * 6...  12.3 us
    all_to_all x2, waiting for transfers between devices, exchange(): return lax.all_to_all(packets, axis, 0, 0, tiled=True).reshape(rows.shape)  11.5 us
    all_to_all x1, blocking collectives, body(): starts = lax.all_to_all(starts, 'core', 0, 0, tiled=True)  7.94 us
    all_to_all x1, blocking collectives, body(): both = lax.all_to_all(summaries, 'core', 0, 0, tiled=True)  5.56 us
    pallas_call x1, Pallas kernels, body(): pl.pallas_call(summary_kernel, grid=(steps,), in_specs=[pl.BlockSpec((1,...  4.17 us
    pallas_call x1, Pallas kernels, body(): pl.pallas_call(final_kernel, in_specs=[whole] * 5, out_specs=[pl.BlockSpe...  3.34 us
  transfers between devices with their start and end apart: 2, of which 2 were waited for; matrix products, arithmetic and copies ran while one was open for 0% of the time, Pallas kernels for 19%

profile of v3, /device:TPU:1, one launch (start us, length us, event | category | flops | bytes accessed | tf_op | source)
XLA Modules:
  0.0 63.8 jit_solution(5842929200332352032)
XLA Ops:
  0.6 4.2 %summary.1 = (f32[2,1040,128]{2,1,0:T(8,128)S(1)}, f32[128,2048]{1,0:T(8,128)}, f32[4,128,128]{2,1,0:T(8,128)}) custom-call(s32[1,256]{1,0:T(1,128)} %bitcast.16, bf16[128,2048]{1,0:T(8,128)(2,1)} %r.5, bf16[128,2048]{1,0:T(8,128)(2,1)} %k.5, bf16[128,2048]{1,0:T(8,128)(2,1)} %v.5, bf16[128,2048]{1,0:T(8,128)(2,1)} %g.5, f32[128,2048]{1,0:T(8,128)} %x.5), custom_call_target="tpu_custom_call" | custom-call | flops 1000000000 | bytes 6000000 | tf_op jit(solution)/shard_map/summary/pallas_call | solution.py:379
  4.8 5.6 %all_to_all.20.got.sums = f32[2,1040,128]{2,1,0:T(8,128)S(1)} all-to-all(f32[2,1040,128]{2,1,0:T(8,128)S(1)} %get-tuple-element.25), channel_id=1, replica_groups=mesh['chip'=64,'core'=2] {'core'}, dimensions={0} | all-to-all | bytes 2129920 | tf_op jit(solution)/shard_map/all_to_all | solution.py:398
  10.4 0.9 %combine.1 = (f32[1152,128]{1,0:T(8,128)}, f32[8,128]{1,0:T(8,128)}) custom-call(f32[2,1040,128]{2,1,0:T(8,128)S(1)} %all_to_all.20.got.sums), custom_call_target="tpu_custom_call" | custom-call | flops 1000000 | bytes 2000000 | tf_op jit(solution)/shard_map/combine/pallas_call | solution.py:399
  11.3 11.2 %all-to-all-start.1 = ((f32[64,18,1,128]{3,2,1,0:T(1,128)}), f32[64,18,1,128]{3,2,1,0:T(1,128)S(1)}, u32[]{:S(2)}, u32[]{:S(2)}) async-start(f32[64,18,1,128]{3,2,1,0:T(1,128)} %bitcast.2), calls=%async_computation.1 | async-start | bytes 1179648 | tf_op jit(solution)/shard_map/all_to_all | solution.py:335
  22.5 6.1 %inside.2 = (f32[1160,1024]{1,0:T(8,128)}, bf16[384,1024]{1,0:T(8,128)(2,1)}, f32[8,128]{1,0:T(8,128)}) custom-call(bf16[128,2048]{1,0:T(8,128)(2,1)} %r.5, bf16[128,2048]{1,0:T(8,128)(2,1)} %k.5, bf16[128,2048]{1,0:T(8,128)(2,1)} %v.5, bf16[128,2048]{1,0:T(8,128)(2,1)} %g.5, f32[128,2048]{1,0:T(8,128)} %x.5, f32[128,2048]{1,0:T(8,128)} %get-tuple-element.23.cum_in, ...), custom_call_target="tpu_custom_call" | custom-call | flops 10000000000 | bytes 10000000 | tf_op jit(solution)/shard_map/inside/pallas_call | solution.py:360
  28.6 6.5 %all-to-all-done.1 = f32[64,18,1,128]{3,2,1,0:T(1,128)S(1)} async-done(((f32[64,18,1,128]{3,2,1,0:T(1,128)}), f32[64,18,1,128]{3,2,1,0:T(1,128)S(1)}, u32[]{:S(2)}, u32[]{:S(2)}) %all-to-all-start.1) | async-done | bytes 589856 | tf_op jit(solution)/shard_map/all_to_all | solution.py:335
  35.2 1.0 %scan.1 = (f32[1088,128]{1,0:T(8,128)}, f32[8,128]{1,0:T(8,128)}) custom-call(f32[1152,128]{1,0:T(8,128)S(1)} %bitcast.11, f32[8,128]{1,0:T(8,128)} %get-tuple-element.30.before), custom_call_target="tpu_custom_call" | custom-call | flops 10000000000 | bytes 30000000 | tf_op jit(solution)/shard_map/scan/pallas_call | solution.py:410
  36.1 5.1 %all-to-all-start.2 = ((f32[64,17,1,128]{3,2,1,0:T(1,128)}), f32[64,17,1,128]{3,2,1,0:T(1,128)S(1)}, u32[]{:S(2)}, u32[]{:S(2)}) async-start(f32[64,17,1,128]{3,2,1,0:T(1,128)} %bitcast.4), calls=%async_computation.2 | async-start | bytes 1114112 | tf_op jit(solution)/shard_map/all_to_all | solution.py:335
  41.2 6.2 %inside.3 = (f32[1160,1024]{1,0:T(8,128)}, bf16[384,1024]{1,0:T(8,128)(2,1)}, f32[8,128]{1,0:T(8,128)}) custom-call(bf16[128,2048]{1,0:T(8,128)(2,1)} %r.5, bf16[128,2048]{1,0:T(8,128)(2,1)} %k.5, bf16[128,2048]{1,0:T(8,128)(2,1)} %v.5, bf16[128,2048]{1,0:T(8,128)(2,1)} %g.5, f32[128,2048]{1,0:T(8,128)} %x.5, f32[128,2048]{1,0:T(8,128)} %get-tuple-element.23.cum_in, ...), custom_call_target="tpu_custom_call" | custom-call | flops 10000000000 | bytes 10000000 | tf_op jit(solution)/shard_map/inside/pallas_call | solution.py:360
  47.4 5.0 %all-to-all-done.2 = f32[64,17,1,128]{3,2,1,0:T(1,128)S(1)} async-done(((f32[64,17,1,128]{3,2,1,0:T(1,128)}), f32[64,17,1,128]{3,2,1,0:T(1,128)S(1)}, u32[]{:S(2)}, u32[]{:S(2)}) %all-to-all-start.2) | async-done | bytes 557088 | tf_op jit(solution)/shard_map/all_to_all | solution.py:335
  52.4 0.0 slice-start
  52.4 0.0 slice-start.2
  52.4 0.0 slice-start.1
  52.4 0.1 expand.1
  52.5 0.0 copy-start
  52.5 0.0 copy-start.1
  52.5 7.9 %all_to_all.21.got = f32[2,1032,128]{2,1,0:T(8,128)S(1)} all-to-all(f32[2,1032,128]{2,1,0:T(8,128)S(1)} %expand.1), channel_id=1, replica_groups=mesh['chip'=64,'core'=2] {'core'}, dimensions={0} | all-to-all | bytes 2113536 | tf_op jit(solution)/shard_map/all_to_all | solution.py:430
  60.4 0.0 slice-done
  60.4 0.0 slice-done.2
  60.4 0.0 slice-done.1
  60.4 0.0 slice-done.3
  60.4 0.0 copy-done
  60.5 0.0 copy-done.1
  60.5 3.3 %final.1 = (bf16[128,2048]{1,0:T(8,128)(2,1)}, bf16[128,2048]{1,0:T(8,128)(2,1)}, bf16[128,2048]{1,0:T(8,128)(2,1)}, bf16[128,2048]{1,0:T(8,128)(2,1)}, f32[1,2048]{1,0:T(1,128)}) custom-call(f32[1160,1024]{1,0:T(8,128)S(1)} %bitcast.8, bf16[384,1024]{1,0:T(8,128)(2,1)S(1)} %copy-done, f32[1160,1024]{1,0:T(8,128)S(1)} %bitcast.10, ...), custom_call_target="tpu_custom_call" | custom-call | flops 1000000000 | bytes 10000000 | tf_op jit(solution)/shard_map/final/pallas_call | solution.py:431
  (3 shorter events, 0.0 us)
Async XLA Ops:
  11.3 23.9 %all-to-all-start.1 = ((f32[64,18,1,128]{3,2,1,0:T(1,128)}), f32[64,18,1,128]{3,2,1,0:T(1,128)S(1)}, u32[]{:S(2)}, u32[]{:S(2)}) async-start(f32[64,18,1,128]{3,2,1,0:T(1,128)} %bitcast.2), calls=%async_computation.1 | async-start | bytes 1179648 | tf_op jit(solution)/shard_map/all_to_all | solution.py:335
  36.1 16.2 %all-to-all-start.2 = ((f32[64,17,1,128]{3,2,1,0:T(1,128)}), f32[64,17,1,128]{3,2,1,0:T(1,128)S(1)}, u32[]{:S(2)}, u32[]{:S(2)}) async-start(f32[64,17,1,128]{3,2,1,0:T(1,128)} %bitcast.4), calls=%async_computation.2 | async-start | bytes 1114112 | tf_op jit(solution)/shard_map/all_to_all | solution.py:335
  52.4 8.1 %slice-start = ((s8[4751360]{0:T(1024)(128)(4,1)}), s8[4194304]{0:T(1024)(128)(4,1)S(1)}, s32[]{:S(2)}) async-start(s8[4751360]{0:T(1024)(128)(4,1)} %bitcast.7), calls=%async_computation.4 | async-start | bytes 8388608
  52.4 8.1 %slice-start.2 = ((s8[4751360]{0:T(1024)(128)(4,1)}), s8[4194304]{0:T(1024)(128)(4,1)S(1)}, s32[]{:S(2)}) async-start(s8[4751360]{0:T(1024)(128)(4,1)} %bitcast.9), calls=%async_computation.6 | async-start | bytes 8388608
  52.4 8.1 %slice-start.1 = ((s8[4751360]{0:T(1024)(128)(4,1)}), s8[557056]{0:T(1024)(128)(4,1)S(1)}, s32[]{:S(2)}) async-start(s8[4751360]{0:T(1024)(128)(4,1)} %bitcast.7), calls=%async_computation.5 | async-start | bytes 1114112
  52.4 8.1 %slice-start.3 = ((s8[4751360]{0:T(1024)(128)(4,1)}), s8[557056]{0:T(1024)(128)(4,1)S(1)}, s32[]{:S(2)}) async-start(s8[4751360]{0:T(1024)(128)(4,1)} %bitcast.9), calls=%async_computation.7 | async-start | bytes 1114112
  52.5 8.0 %copy-start = (bf16[384,1024]{1,0:T(8,128)(2,1)S(1)}, bf16[384,1024]{1,0:T(8,128)(2,1)}, u32[]{:S(2)}) copy-start(bf16[384,1024]{1,0:T(8,128)(2,1)} %get-tuple-element.28.narrow_a) | copy-start | bytes 2359300
  52.5 8.0 %copy-start.1 = (bf16[384,1024]{1,0:T(8,128)(2,1)S(1)}, bf16[384,1024]{1,0:T(8,128)(2,1)}, u32[]{:S(2)}) copy-start(bf16[384,1024]{1,0:T(8,128)(2,1)} %get-tuple-element.33.narrow_b) | copy-start | bytes 2359300

commit v4 on v3

--- a/solution.py
+++ b/solution.py
@@ -99,35 +99,42 @@
     return jnp.exp2(x * LOG2_E + LOG2_LOG2_E)
 
 
-def summary_kernel(spans, r, k, v, g, x, out, cum_out, masks_out, keep, carried, passes):
+def mark_segments(spans, marks):
+    rank = lax.axis_index("chip") * CORES + lax.axis_index("core")
+    seg_across, seg_down, prev = segments(spans[...], rank * TOK)
+    row, col = square()
+    same = seg_down == seg_across
+    last = seg_down[TOK - 1 :]
+    marks[0] = (same & (row > col)).astype(F32)
+    marks[1] = (same & (row < col)).astype(F32)
+    marks[2] = jnp.broadcast_to((seg_down == last).astype(F32), (TOK, LANES))
+    marks[3] = jnp.broadcast_to((seg_down == prev).astype(F32), (TOK, LANES))
+
+
+def running_sum(speeds):
+    row, col = square()
+    lower = (row >= col).astype(F32).astype(BF16)
+    return dot(cat(lower, lower, axis=1), cat(*halves(speeds), axis=0), NN)
+
+
+def summary_kernel(spans, r, k, v, g, x, mine, theirs, cums, marks, out):
     @pl.when(pl.program_id(0) == 0)
     def _():
-        seg_across, seg_down, prev = segments(spans[...], (lax.axis_index("chip") * CORES + lax.axis_index("core")) * TOK)
-        row, col = square()
-        same = seg_down == seg_across
-        last = seg_down[TOK - 1 :]
-        keep[...] = jnp.broadcast_to((seg_down == last).astype(F32), (TOK, LANES))
-        carried[...] = jnp.broadcast_to((seg_down == prev).astype(F32), (TOK, LANES))
-        passes[...] = jnp.broadcast_to((last == prev).astype(F32), passes.shape)
-        masks_out[0] = (same & (row > col)).astype(F32)
-        masks_out[1] = (same & (row < col)).astype(F32)
-        masks_out[2] = keep[...]
-        masks_out[3] = carried[...]
-
-    row, col = square()
-    lower = (row >= col).astype(F32).astype(BF16)
-    lower = cat(lower, lower, axis=1)
+        mark_segments(spans, marks)
+
+    keep, carried = marks.at[2], marks.at[3]
+    passes = marks[2, TOK - 1 :] * marks[3, TOK - 1 :]
     ones = ones_by_head()
     lane = lax.broadcasted_iota(jnp.int32, (HS, LANES), 1)
     spots = [slice(pair * LANES, (pair + 1) * LANES) for pair in range(PAIRS)]
     for group in range(0, PAIRS, GROUP):
         wide = slice(group * LANES, (group + GROUP) * LANES)
-        cum_out[:, wide] = dot(lower, cat(*halves(decay_rate(x[:, wide])), axis=0), NN)
+        cums[:, wide] = running_sum(decay_rate(x[:, wide]))
     products = [cat(*halves(g[:, at].astype(F32) * v[:, at].astype(F32)), axis=1) for at in spots]
     bonuses = dot(cat(*products, axis=0), ones, NN)
     endings, reaches = [], []
     for at in spots:
-        cum = cum_out[:, at]
+        cum = cums[:, at]
         rp, kp = r[:, at].astype(F32), k[:, at].astype(F32)
         ending = kp * jnp.exp2(cum - cum[TOK - 1 :]) * keep[...]
         reached = rp * jnp.exp2(decay_rate(x[:, at]) - cum) * carried[...]
@@ -139,24 +146,39 @@
         for place, both in ((0, ends[pair]), (PULL, pulls[pair])):
             both = both[:, :LANES] + both[:, LANES:]
             state = jnp.where(lane < HS, both[:HS], both[HS:])
-            out[0, place + pair * HS : place + (pair + 1) * HS] = state
+            out[place + pair * HS : place + (pair + 1) * HS] = state
         bonus = r[:, at].astype(F32) * k[:, at].astype(F32) * bonuses[pair * TOK : (pair + 1) * TOK]
-        through = jnp.exp2(-cum_out[TOK - 1 :, at]) * passes[:1]
-        out[0, DECAY + pair : DECAY + pair + 1] = through
-        out[0, BONUS + pair : BONUS + pair + 1] = jnp.sum(bonus, axis=0, keepdims=True)
-
-
-def combine_kernel(got, out, done):
+        through = jnp.exp2(-cums[TOK - 1 :, at]) * passes
+        out[DECAY + pair : DECAY + pair + 1] = through
+        out[BONUS + pair : BONUS + pair + 1] = jnp.sum(bonus, axis=0, keepdims=True)
+    ours = pl.program_id(0) == lax.axis_index("core")
+    for condition, target in ((ours, mine), (jnp.logical_not(ours), theirs)):
+
+        @pl.when(condition)
+        def _():
+            target[...] = out[...]
+
+
+def in_order(mine, theirs):
+    first = lax.axis_index("core") == 0
+
+    def load(rows):
+        own, other = mine[rows], theirs[rows]
+        return jnp.where(first, own, other), jnp.where(first, other, own)
+
+    return load
+
+
+def combine_kernel(mine, theirs, out, done):
     done[...] = jnp.zeros(done.shape, F32)
-    first, second = got.at[0], got.at[1]
+    load = in_order(mine, theirs)
     for pair in range(HALF):
-        rows = slice(pair * HS, (pair + 1) * HS)
-        below = slice(PULL + pair * HS, PULL + (pair + 1) * HS)
-        near = first[DECAY + pair : DECAY + pair + 1]
-        far = second[DECAY + pair : DECAY + pair + 1]
-        ends = far * first[rows] + second[rows]
-        pulls = first[below] + near * second[below]
-        bonus = first[BONUS + pair : BONUS + pair + 1] + second[BONUS + pair : BONUS + pair + 1]
+        first_end, second_end = load(slice(pair * HS, (pair + 1) * HS))
+        first_pull, second_pull = load(slice(PULL + pair * HS, PULL + (pair + 1) * HS))
+        near, far = load(slice(DECAY + pair, DECAY + pair + 1))
+        ends = far * first_end + second_end
+        pulls = first_pull + near * second_pull
+        bonus = sum(load(slice(BONUS + pair, BONUS + pair + 1)))
         rest = cat(near * far, bonus, axis=0)
         for peer in range(BLOCKS):
             at = (pair * BLOCKS + peer) * ROWS_OUT
@@ -166,9 +188,10 @@
             out[at + 2 * STATE_ROWS : at + ROWS_OUT] = rest
 
 
-def expand_kernel(got, sums, before, out):
+def expand_kernel(got, mine, theirs, before, own, other):
     del before
-    first, second = sums.at[0], sums.at[1]
+    load = in_order(mine, theirs)
+    first = lax.axis_index("core") == 0
     for pair in range(HALF):
         rows = slice(pair * HS, (pair + 1) * HS)
         below = slice(PULL + pair * HS, PULL + (pair + 1) * HS)
@@ -176,14 +199,15 @@
         state = cat(*(got[row : row + STATE_ROWS] for row in starts), axis=0)
         dstate = cat(*(got[row + STATE_ROWS : row + 2 * STATE_ROWS] for row in starts), axis=0)
         bonus = got[starts[0] + 2 * STATE_ROWS : starts[0] + ROWS_BACK]
-        near = first[DECAY + pair : DECAY + pair + 1]
-        far = second[DECAY + pair : DECAY + pair + 1]
-        out[0, rows] = state
-        out[0, below] = far * dstate + second[below]
-        out[1, rows] = near * state + first[rows]
-        out[1, below] = dstate
-        for core in range(CORES):
-            out[core, DECAY + pair : DECAY + pair + 1] = bonus
+        near, far = load(slice(DECAY + pair, DECAY + pair + 1))
+        second_state = near * state + load(rows)[0]
+        first_dstate = far * dstate + load(below)[1]
+        own[rows] = jnp.where(first, state, second_state)
+        other[rows] = jnp.where(first, second_state, state)
+        own[below] = jnp.where(first, first_dstate, dstate)
+        other[below] = jnp.where(first, dstate, first_dstate)
+        for out in (own, other):
+            out[DECAY + pair : DECAY + pair + 1] = bonus
 
 
 def scan_kernel(got, before, out, done):
@@ -207,8 +231,13 @@
         state = through * state + got[at + STATE_ROWS : at + 2 * STATE_ROWS]
 
 
-def inside_kernel(r, k, v, g, x, cum_in, u, masks, combined, full_out, half_out, done):
-    del combined
+def inside_kernel(spans, r, k, v, g, x, u, before, full_out, half_out, done, cums, masks):
+    del before
+
+    @pl.when(pl.program_id(0) == 0)
+    def _():
+        mark_segments(spans, masks)
+
     done[...] = jnp.zeros(done.shape, F32)
     dr, dk, dv, dl, rd, kd, pr, pk, rate = (full_out.at[rows] for rows in FULL_ROWS)
     el, gc, vc = (half_out.at[rows] for rows in HALF_ROWS)
@@ -223,10 +252,11 @@
     later = cat(masks[1], masks[1], axis=1) > 0.0
     both = masks[2][TOK - 1 :] * masks[3][TOK - 1 :]
     spots = [slice(pair * LANES, (pair + 1) * LANES) for pair in range(r.shape[1] // LANES)]
+    cums[...] = running_sum(decay_rate(x[...]))
     scaled, products = [], []
     for at in spots:
         rp, kp, vp, gp = (part[:, at].astype(F32) for part in (r, k, v, g))
-        cum = cum_in[:, at]
+        cum = cums[:, at]
         last = cum[TOK - 1 :]
         middle = 0.5 * last
         speed = decay_rate(x[:, at])
@@ -275,12 +305,14 @@
         dl[:, at] = part[:, :LANES] + part[:, LANES:]
 
 
-def final_kernel(full_a, narrow_a, full_b, narrow_b, got, dr, dk, dv, dx, du, rounded, sems):
+def final_kernel(full_a, narrow_a, full_b, narrow_b, mine, theirs, dr, dk, dv, dx, du, rounded, sems):
     heads = head_masks()
     row, col = square()
     after = (row < col).astype(F32).astype(BF16)
     earlier = (row > col).astype(F32).astype(BF16)
     sums = cat(after, earlier, axis=1)
+    load = in_order(mine, theirs)
+    got = (lambda rows: load(rows)[0], lambda rows: load(rows)[1])
     copies = []
     for base in range(0, du.shape[1] // LANES, WRITE):
         half = base // HALF
@@ -292,9 +324,9 @@
         targets = [slice(pair * LANES, (pair + 1) * LANES) for pair in range(base, base + WRITE)]
         loaded, across = [], []
         for place, at, to in zip(places, spots, targets):
-            state = got[half, place * HS : (place + 1) * HS]
-            dstate = got[half, PULL + place * HS : PULL + (place + 1) * HS]
-            du[:, to] = got[half, DECAY + place : DECAY + place + 1]
+            state = got[half](slice(place * HS, (place + 1) * HS))
+            dstate = got[half](slice(PULL + place * HS, PULL + (place + 1) * HS))
+            du[:, to] = got[half](slice(DECAY + place, DECAY + place + 1))
             loaded.append([by_head(part, heads) for part in halves(state) + halves(dstate)])
             across.append(full[FULL_TOK : FULL_TOK + 1, at] * jnp.sum(state * dstate, axis=0, keepdims=True))
         reaches, pulls, values = [], [], []
@@ -330,6 +362,10 @@
     return pltpu.with_memory_space_constraint(x, pltpu.VMEM)
 
 
+def swap(rows):
+    return lax.ppermute(rows, "core", [(0, 1), (1, 0)])
+
+
 def exchange(rows, peers, axis):
     packets = rows.reshape(peers, -1, 1, LANES)
     return lax.all_to_all(packets, axis, 0, 0, tiled=True).reshape(rows.shape)
@@ -339,12 +375,8 @@
     tokens, width = r.shape
     npairs = width // LANES
     chips = lax.axis_size("chip")
-    steps = npairs // PAIRS
-    part = PAIRS * LANES
     r, k, v, x, g, u = (hbm(part) for part in (r, k, v, x, g, u.reshape(1, -1)))
-    wide = pl.BlockSpec((TOK, part), lambda i: (0, i))
-    thin = pl.BlockSpec((1, part), lambda i: (0, i))
-    fixed = pl.BlockSpec((4, TOK, LANES), lambda i: (0, 0, 0))
+    spans = hbm(spans.reshape(1, -1))
     whole = pl.BlockSpec(memory_space=pltpu.VMEM)
     token = pl.BlockSpec(memory_space=pl.ANY)
     params = pltpu.CompilerParams(vmem_limit_bytes=VMEM)
@@ -360,7 +392,7 @@
         return pl.pallas_call(
             inside_kernel,
             grid=(HALF // INSIDE,),
-            in_specs=[wide] * 6 + [pl.BlockSpec((1, part), lambda i: (0, i + here)), fixed, token],
+            in_specs=[whole] + [wide] * 5 + [pl.BlockSpec((1, part), lambda i: (0, i + here)), token],
             out_specs=[
                 pl.BlockSpec((FULL_TOK + 8, part), lambda i: (0, i)),
                 pl.BlockSpec((3 * TOK, part), lambda i: (0, i)),
@@ -371,40 +403,39 @@
                 pltpu.HBM((3 * TOK, HALF * LANES), BF16),
                 pltpu.HBM((8, LANES), F32),
             ],
+            scratch_shapes=[pltpu.VMEM((TOK, part), F32), pltpu.VMEM((4, TOK, LANES), F32)],
             name="inside",
             compiler_params=params,
             cost_estimate=cost(10**10, 10**7),
-        )(r, k, v, g, x, hbm(cum), u, hbm(masks), hbm(after))
-
-    summaries, cum, masks = pl.pallas_call(
+        )(spans, r, k, v, g, x, u, hbm(after))
+
+    part = PAIRS * LANES
+    block = (BONUS + HALF, LANES)
+    mine, theirs = pl.pallas_call(
         summary_kernel,
-        grid=(steps,),
-        in_specs=[pl.BlockSpec((1, spans.shape[0]), lambda i: (0, 0))] + [wide] * 5,
-        out_specs=[pl.BlockSpec((1, BONUS + HALF, LANES), lambda i: (i, 0, 0)), wide, fixed],
+        grid=(width // part,),
+        in_specs=[whole] + [pl.BlockSpec((TOK, part), lambda i: (0, i))] * 5,
+        out_specs=[whole] * 2,
+        out_shape=[jax.ShapeDtypeStruct(block, F32)] * 2,
         scratch_shapes=[
-            pltpu.VMEM((TOK, LANES), F32),
-            pltpu.VMEM((TOK, LANES), F32),
-            pltpu.VMEM((8, LANES), F32),
-        ],
-        out_shape=[
-            jax.ShapeDtypeStruct((CORES, BONUS + HALF, LANES), F32),
-            pltpu.HBM((tokens, width), F32),
-            pltpu.HBM((4, TOK, LANES), F32),
+            pltpu.VMEM((TOK, part), F32),
+            pltpu.VMEM((4, TOK, LANES), F32),
+            pltpu.VMEM(block, F32),
         ],
         name="summary",
         compiler_params=params,
         cost_estimate=cost(10**9, 6 * 10**6),
-    )(hbm(spans.reshape(1, -1)), r, k, v, g, x)
-    both = lax.all_to_all(summaries, "core", 0, 0, tiled=True)
+    )(spans, r, k, v, g, x)
+    theirs = swap(theirs)
     packets, combined = pl.pallas_call(
         combine_kernel,
-        in_specs=[whole],
+        in_specs=[whole] * 2,
         out_specs=[whole, whole],
         out_shape=[jax.ShapeDtypeStruct((chips * ROWS_OUT, LANES), F32), pltpu.HBM((8, LANES), F32)],
         name="combine",
         compiler_params=params,
         cost_estimate=cost(10**6, 2 * 10**6),
-    )(both)
+    )(mine, theirs)
     got = exchange(packets, chips, "chip")
     first, narrow_first, done = inside(0, combined)
     states, scanned = pl.pallas_call(
@@ -418,19 +449,19 @@
     )(vm(got), hbm(done))
     returned = exchange(states, chips, "chip")
     second, narrow_second, done = inside(1, scanned)
-    starts = pl.pallas_call(
+    own, other = pl.pallas_call(
         expand_kernel,
-        in_specs=[whole, whole, token],
-        out_specs=whole,
-        out_shape=jax.ShapeDtypeStruct((CORES, BONUS, LANES), F32),
+        in_specs=[whole, whole, whole, token],
+        out_specs=[whole] * 2,
+        out_shape=[jax.ShapeDtypeStruct((BONUS, LANES), F32)] * 2,
         name="expand",
         compiler_params=params,
         cost_estimate=cost(10**10, 3 * 10**7),
-    )(returned, both, hbm(done))
-    starts = lax.all_to_all(starts, "core", 0, 0, tiled=True)
+    )(returned, mine, theirs, hbm(done))
+    other = swap(other)
     dr, dk, dv, dx, du = pl.pallas_call(
         final_kernel,
-        in_specs=[whole] * 5,
+        in_specs=[whole] * 6,
         out_specs=[pl.BlockSpec(memory_space=pl.ANY)] * 4 + [whole],
         out_shape=[pltpu.HBM((tokens, width), BF16)] * 4 + [jax.ShapeDtypeStruct((1, width), F32)],
         scratch_shapes=[
@@ -440,7 +471,7 @@
         name="final",
         compiler_params=params,
         cost_estimate=cost(10**9, 10**7),
-    )(vm(first), vm(narrow_first), vm(second), vm(narrow_second), vm(starts))
+    )(vm(first), vm(narrow_first), vm(second), vm(narrow_second), vm(own), vm(other))
     return dr, dk, dv, dx, du.reshape(width)
 
 

time: 64.2 us -> 58.7 us (0.914); the launches traced: 63.8 us -> 57.6 us
  blocking collectives: 13.5 us -> 0 us
  starting transfers between devices: 16.3 us -> 21.1 us
  waiting for transfers between devices: 11.5 us -> 14 us
    all_to_all x2 -> x0, blocking collectives: 13.5 us -> none  [the longest x1 7.94 us: body(): starts = lax.all_to_all(starts, 'core', 0, 0, tiled=True)]
    ppermute x0 -> x2, starting transfers between devices: none -> 4.77 us  [swap(): return lax.ppermute(rows, 'core', [(0, 1), (1, 0)])]
    ppermute x0 -> x2, waiting for transfers between devices: none -> 3.09 us  [swap(): return lax.ppermute(rows, 'core', [(0, 1), (1, 0)])]
  transfers between devices with their start and end apart: 2 -> 4, of which waited for: 2 -> 4; matrix products, arithmetic and copies ran while one was open for 0% -> 0% of each run, Pallas kernels for 19% -> 22%
where the time goes in v4:
time: 58.7 us; the launch traced here: 57.6 us
  Pallas kernels  21.8 us (37%)
  starting transfers between devices  21.1 us (36%)
  waiting for transfers between devices  14 us (24%)
  between operations  0.7 us (1%)
    all_to_all x2, starting transfers between devices, exchange(): return lax.all_to_all(packets, axis, 0, 0, tiled=True).reshape(rows.shape)  16.3 us
    pallas_call x2, Pallas kernels, inside(): pl.pallas_call(inside_kernel, grid=(HALF // INSIDE,), in_specs=[whole] +...  12.9 us
    all_to_all x2, waiting for transfers between devices, exchange(): return lax.all_to_all(packets, axis, 0, 0, tiled=True).reshape(rows.shape)  10.9 us
    ppermute x2, starting transfers between devices, swap(): return lax.ppermute(rows, 'core', [(0, 1), (1, 0)])  4.77 us
    pallas_call x1, Pallas kernels, body(): pl.pallas_call(summary_kernel, grid=(width // part,), in_specs=[whole] +...  3.56 us
    pallas_call x1, Pallas kernels, body(): pl.pallas_call(final_kernel, in_specs=[whole] * 6, out_specs=[pl.BlockSpe...  3.35 us
    ppermute x2, waiting for transfers between devices, swap(): return lax.ppermute(rows, 'core', [(0, 1), (1, 0)])  3.09 us
  transfers between devices with their start and end apart: 4, of which 4 were waited for; matrix products, arithmetic and copies ran while one was open for 0% of the time, Pallas kernels for 22%

profile of v4, /device:TPU:1, one launch (start us, length us, event | category | flops | bytes accessed | tf_op | source)
XLA Modules:
  0.0 57.6 jit_solution(5543047181474525274)
XLA Ops:
  0.6 3.6 %summary.1 = (f32[1040,128]{1,0:T(8,128)S(1)}, f32[1040,128]{1,0:T(8,128)S(1)}) custom-call(s32[1,256]{1,0:T(1,128)} %bitcast.14, bf16[128,2048]{1,0:T(8,128)(2,1)} %r.5, bf16[128,2048]{1,0:T(8,128)(2,1)} %k.5, bf16[128,2048]{1,0:T(8,128)(2,1)} %v.5, bf16[128,2048]{1,0:T(8,128)(2,1)} %g.5, f32[128,2048]{1,0:T(8,128)} %x.5), custom_call_target="tpu_custom_call" | custom-call | flops 1000000000 | bytes 6000000 | tf_op jit(solution)/shard_map/summary/pallas_call | solution.py:414
  4.2 1.5 %collective-permute-start = (f32[1040,128]{1,0:T(8,128)S(1)}, f32[1040,128]{1,0:T(8,128)S(1)}, u32[]{:S(2)}, u32[]{:S(2)}) collective-permute-start(f32[1040,128]{1,0:T(8,128)S(1)} %get-tuple-element.25), channel_id=1, source_target_pairs={{0,1},{1,0},{2,3},{3,2},{4,5},{5,4},{6,7},{7,6},{8,9},{9,8},{10,11... | collective-permute-start | bytes 1597448 | tf_op jit(solution)/shard_map/ppermute | solution.py:366
  5.7 1.5 %collective-permute-done.theirs = f32[1040,128]{1,0:T(8,128)S(1)} collective-permute-done((f32[1040,128]{1,0:T(8,128)S(1)}, f32[1040,128]{1,0:T(8,128)S(1)}, u32[]{:S(2)}, u32[]{:S(2)}) %collective-permute-start) | collective-permute-done | bytes 532512 | tf_op jit(solution)/shard_map/ppermute | solution.py:366
  7.2 0.9 %combine.1 = (f32[1152,128]{1,0:T(8,128)}, f32[8,128]{1,0:T(8,128)}) custom-call(f32[1040,128]{1,0:T(8,128)S(1)} %get-tuple-element.24.mine, f32[1040,128]{1,0:T(8,128)S(1)} %collective-permute-done.theirs), custom_call_target="tpu_custom_call" | custom-call | flops 1000000 | bytes 2000000 | tf_op jit(solution)/shard_map/combine/pallas_call | solution.py:430
  8.1 11.2 %all-to-all-start = ((f32[64,18,1,128]{3,2,1,0:T(1,128)}), f32[64,18,1,128]{3,2,1,0:T(1,128)S(1)}, u32[]{:S(2)}, u32[]{:S(2)}) async-start(f32[64,18,1,128]{3,2,1,0:T(1,128)} %bitcast.2), calls=%async_computation | async-start | bytes 1179648 | tf_op jit(solution)/shard_map/all_to_all | solution.py:371
  19.4 6.4 %inside.2 = (f32[1160,1024]{1,0:T(8,128)}, bf16[384,1024]{1,0:T(8,128)(2,1)}, f32[8,128]{1,0:T(8,128)}) custom-call(s32[1,256]{1,0:T(1,128)} %bitcast.15, bf16[128,2048]{1,0:T(8,128)(2,1)} %r.5, bf16[128,2048]{1,0:T(8,128)(2,1)} %k.5, bf16[128,2048]{1,0:T(8,128)(2,1)} %v.5, bf16[128,2048]{1,0:T(8,128)(2,1)} %g.5, f32[128,2048]{1,0:T(8,128)} %x.5, ...), custom_call_target="tpu_custom_call" | custom-call | flops 10000000000 | bytes 10000000 | tf_op jit(solution)/shard_map/inside/pallas_call | solution.py:392
  25.8 6.2 %all-to-all-done = f32[64,18,1,128]{3,2,1,0:T(1,128)S(1)} async-done(((f32[64,18,1,128]{3,2,1,0:T(1,128)}), f32[64,18,1,128]{3,2,1,0:T(1,128)S(1)}, u32[]{:S(2)}, u32[]{:S(2)}) %all-to-all-start) | async-done | bytes 589856 | tf_op jit(solution)/shard_map/all_to_all | solution.py:371
  32.0 1.0 %scan.1 = (f32[1088,128]{1,0:T(8,128)}, f32[8,128]{1,0:T(8,128)}) custom-call(f32[1152,128]{1,0:T(8,128)S(1)} %bitcast.9, f32[8,128]{1,0:T(8,128)} %get-tuple-element.30.before), custom_call_target="tpu_custom_call" | custom-call | flops 10000000000 | bytes 30000000 | tf_op jit(solution)/shard_map/scan/pallas_call | solution.py:441
  33.0 5.1 %all-to-all-start.1 = ((f32[64,17,1,128]{3,2,1,0:T(1,128)}), f32[64,17,1,128]{3,2,1,0:T(1,128)S(1)}, u32[]{:S(2)}, u32[]{:S(2)}) async-start(f32[64,17,1,128]{3,2,1,0:T(1,128)} %bitcast.4), calls=%async_computation.1 | async-start | bytes 1114112 | tf_op jit(solution)/shard_map/all_to_all | solution.py:371
  38.1 0.0 slice-start
  38.1 6.5 %inside.3 = (f32[1160,1024]{1,0:T(8,128)}, bf16[384,1024]{1,0:T(8,128)(2,1)}, f32[8,128]{1,0:T(8,128)}) custom-call(s32[1,256]{1,0:T(1,128)} %bitcast.16, bf16[128,2048]{1,0:T(8,128)(2,1)} %r.5, bf16[128,2048]{1,0:T(8,128)(2,1)} %k.5, bf16[128,2048]{1,0:T(8,128)(2,1)} %v.5, bf16[128,2048]{1,0:T(8,128)(2,1)} %g.5, f32[128,2048]{1,0:T(8,128)} %x.5, ...), custom_call_target="tpu_custom_call" | custom-call | flops 10000000000 | bytes 10000000 | tf_op jit(solution)/shard_map/inside/pallas_call | solution.py:392
  44.6 4.7 %all-to-all-done.1 = f32[64,17,1,128]{3,2,1,0:T(1,128)S(1)} async-done(((f32[64,17,1,128]{3,2,1,0:T(1,128)}), f32[64,17,1,128]{3,2,1,0:T(1,128)S(1)}, u32[]{:S(2)}, u32[]{:S(2)}) %all-to-all-start.1) | async-done | bytes 557088 | tf_op jit(solution)/shard_map/all_to_all | solution.py:371
  49.2 0.0 slice-start.1
  49.2 0.0 copy-start.1
  49.2 0.0 copy-start.2
  49.3 0.1 expand.1
  49.4 3.3 %collective-permute-start.1 = (f32[1032,128]{1,0:T(8,128)S(1)}, f32[1032,128]{1,0:T(8,128)S(1)}, u32[]{:S(2)}, u32[]{:S(2)}) collective-permute-start(f32[1032,128]{1,0:T(8,128)S(1)} %get-tuple-element.37), channel_id=1, source_target_pairs={{0,1},{1,0},{2,3},{3,2},{4,5},{5,4},{6,7},{7,6},{8,9},{9,8},{10,11... | collective-permute-start | bytes 1585160 | tf_op jit(solution)/shard_map/ppermute | solution.py:366
  52.7 1.5 %collective-permute-done.1.theirs = f32[1032,128]{1,0:T(8,128)S(1)} collective-permute-done((f32[1032,128]{1,0:T(8,128)S(1)}, f32[1032,128]{1,0:T(8,128)S(1)}, u32[]{:S(2)}, u32[]{:S(2)}) %collective-permute-start.1) | collective-permute-done | bytes 528416 | tf_op jit(solution)/shard_map/ppermute | solution.py:366
  54.2 0.0 slice-done
  54.2 0.0 slice-done.1
  54.3 0.0 copy-done
  54.3 0.0 copy-done.1
  54.3 0.0 copy-done.2
  54.3 3.4 %final.1 = (bf16[128,2048]{1,0:T(8,128)(2,1)}, bf16[128,2048]{1,0:T(8,128)(2,1)}, bf16[128,2048]{1,0:T(8,128)(2,1)}, bf16[128,2048]{1,0:T(8,128)(2,1)}, f32[1,2048]{1,0:T(1,128)}) custom-call(f32[1160,1024]{1,0:T(8,128)S(1)} %bitcast.8, bf16[384,1024]{1,0:T(8,128)(2,1)S(1)} %copy-done.1, f32[1160,1024]{1,0:T(8,128)S(1)} %copy-done, ...), custom_call_target="tpu_custom_call" | custom-call | flops 1000000000 | bytes 10000000 | tf_op jit(solution)/shard_map/final/pallas_call | solution.py:462
  (2 shorter events, 0.0 us)
Async XLA Ops:
  4.2 3.0 %collective-permute-start = (f32[1040,128]{1,0:T(8,128)S(1)}, f32[1040,128]{1,0:T(8,128)S(1)}, u32[]{:S(2)}, u32[]{:S(2)}) collective-permute-start(f32[1040,128]{1,0:T(8,128)S(1)} %get-tuple-element.25), channel_id=1, source_target_pairs={{0,1},{1,0},{2,3},{3,2},{4,5},{5,4},{6,7},{7,6},{8,9},{9,8},{10,11... | collective-permute-start | bytes 1597448 | tf_op jit(solution)/shard_map/ppermute | solution.py:366
  8.1 23.9 %all-to-all-start = ((f32[64,18,1,128]{3,2,1,0:T(1,128)}), f32[64,18,1,128]{3,2,1,0:T(1,128)S(1)}, u32[]{:S(2)}, u32[]{:S(2)}) async-start(f32[64,18,1,128]{3,2,1,0:T(1,128)} %bitcast.2), calls=%async_computation | async-start | bytes 1179648 | tf_op jit(solution)/shard_map/all_to_all | solution.py:371
  33.0 16.2 %all-to-all-start.1 = ((f32[64,17,1,128]{3,2,1,0:T(1,128)}), f32[64,17,1,128]{3,2,1,0:T(1,128)S(1)}, u32[]{:S(2)}, u32[]{:S(2)}) async-start(f32[64,17,1,128]{3,2,1,0:T(1,128)} %bitcast.4), calls=%async_computation.1 | async-start | bytes 1114112 | tf_op jit(solution)/shard_map/all_to_all | solution.py:371
  38.1 16.2 %slice-start = ((s8[4751360]{0:T(1024)(128)(4,1)}), s8[557056]{0:T(1024)(128)(4,1)S(1)}, s32[]{:S(2)}) async-start(s8[4751360]{0:T(1024)(128)(4,1)} %bitcast.7), calls=%async_computation.2 | async-start | bytes 1114112
  49.2 5.0 %slice-start.1 = ((s8[4751360]{0:T(1024)(128)(4,1)}), s8[4194304]{0:T(1024)(128)(4,1)S(1)}, s32[]{:S(2)}) async-start(s8[4751360]{0:T(1024)(128)(4,1)} %bitcast.7), calls=%async_computation.3 | async-start | bytes 8388608
  49.2 5.0 %copy-start = (f32[1160,1024]{1,0:T(8,128)S(1)}, f32[1160,1024]{1,0:T(8,128)}, u32[]{:S(2)}) copy-start(f32[1160,1024]{1,0:T(8,128)} %get-tuple-element.32.full_b) | copy-start | bytes 14254084
  49.2 5.0 %copy-start.1 = (bf16[384,1024]{1,0:T(8,128)(2,1)S(1)}, bf16[384,1024]{1,0:T(8,128)(2,1)}, u32[]{:S(2)}) copy-start(bf16[384,1024]{1,0:T(8,128)(2,1)} %get-tuple-element.28.narrow_a) | copy-start | bytes 2359300
  49.2 5.0 %copy-start.2 = (bf16[384,1024]{1,0:T(8,128)(2,1)S(1)}, bf16[384,1024]{1,0:T(8,128)(2,1)}, u32[]{:S(2)}) copy-start(bf16[384,1024]{1,0:T(8,128)(2,1)} %get-tuple-element.33.narrow_b) | copy-start | bytes 2359300
  49.4 4.9 %collective-permute-start.1 = (f32[1032,128]{1,0:T(8,128)S(1)}, f32[1032,128]{1,0:T(8,128)S(1)}, u32[]{:S(2)}, u32[]{:S(2)}) collective-permute-start(f32[1032,128]{1,0:T(8,128)S(1)} %get-tuple-element.37), channel_id=1, source_target_pairs={{0,1},{1,0},{2,3},{3,2},{4,5},{5,4},{6,7},{7,6},{8,9},{9,8},{10,11... | collective-permute-start | bytes 1585160 | tf_op jit(solution)/shard_map/ppermute | solution.py:366

commit v5 on v4

--- a/solution.py
+++ b/solution.py
@@ -29,9 +29,8 @@
 F32 = jnp.float32
 BF16 = jnp.bfloat16
 
-FULL_ROWS = [slice(n * TOK, (n + 1) * TOK) for n in range(9)]
-FULL_TOK = 9 * TOK
-HALF_ROWS = [slice(n * TOK, (n + 1) * TOK) for n in range(3)]
+FULL_ROWS = [slice(n * TOK, (n + 1) * TOK) for n in range(7)]
+FULL_TOK = 7 * TOK
 
 NN = (((1,), (0,)), ((), ()))
 NT = (((1,), (1,)), ((), ()))
@@ -231,7 +230,7 @@
         state = through * state + got[at + STATE_ROWS : at + 2 * STATE_ROWS]
 
 
-def inside_kernel(spans, r, k, v, g, x, u, before, full_out, half_out, done, cums, masks):
+def inside_kernel(spans, r, k, v, g, x, u, before, full_out, kept, done, cums, masks):
     del before
 
     @pl.when(pl.program_id(0) == 0)
@@ -239,8 +238,7 @@
         mark_segments(spans, masks)
 
     done[...] = jnp.zeros(done.shape, F32)
-    dr, dk, dv, dl, rd, kd, pr, pk, rate = (full_out.at[rows] for rows in FULL_ROWS)
-    el, gc, vc = (half_out.at[rows] for rows in HALF_ROWS)
+    dr, dk, dv, dl, rd, kd, rate = (full_out.at[rows] for rows in FULL_ROWS)
     through = full_out.at[FULL_TOK:]
     heads = head_masks()
     ones = ones_by_head()
@@ -264,18 +262,12 @@
         scale_k = jnp.exp2(cum - middle)
         scaled.append((scale_r, scale_k, halves(rp * scale_r), halves(kp * scale_k)))
         products += [cat(*halves(rp * u[:, at] * kp), axis=1), cat(*halves(gp * vp), axis=1)]
-        reached = jnp.exp2(speed - cum) * masks[3]
-        kept = jnp.exp2(cum - last) * masks[2]
-        rd[:, at] = reached
-        kd[:, at] = kept
-        pr[:, at] = rp * reached
-        ending = kp * kept
-        pk[:, at] = ending
-        el[:, at] = halves(ending)[1]
+        rd[:, at] = jnp.exp2(speed - cum) * masks[3]
+        kd[:, at] = jnp.exp2(cum - last) * masks[2]
         rate[:, at] = -LN_2 * speed
         through[:, at] = jnp.broadcast_to(jnp.exp2(-last) * both, (8, LANES))
-        gc[:, at] = g[:, at]
-        vc[:, at] = v[:, at]
+        for n, stream in enumerate((r, k, v, g)):
+            kept[n * TOK : (n + 1) * TOK, at] = stream[:, at]
     own = dot(cat(*products, axis=0), ones, NN)
     pulls, scores = [], []
     for at, (_, _, (rh, rl), (kh, kl)) in zip(spots, scaled):
@@ -305,7 +297,7 @@
         dl[:, at] = part[:, :LANES] + part[:, LANES:]
 
 
-def final_kernel(full_a, narrow_a, full_b, narrow_b, mine, theirs, dr, dk, dv, dx, du, rounded, sems):
+def final_kernel(full_a, kept_a, full_b, kept_b, mine, theirs, dr, dk, dv, dx, du, rounded, sems):
     heads = head_masks()
     row, col = square()
     after = (row < col).astype(F32).astype(BF16)
@@ -316,9 +308,9 @@
     copies = []
     for base in range(0, du.shape[1] // LANES, WRITE):
         half = base // HALF
-        full, narrow = ((full_a, narrow_a), (full_b, narrow_b))[half]
-        dri, dki, dvi, dli, rd, kd, pr, pk, rate = (full.at[rows] for rows in FULL_ROWS)
-        el_in, g, v = (narrow.at[rows] for rows in HALF_ROWS)
+        full, kept = ((full_a, kept_a), (full_b, kept_b))[half]
+        r, k, v, g = (kept.at[n * TOK : (n + 1) * TOK] for n in range(4))
+        dri, dki, dvi, dli, rd, kd, rate = (full.at[rows] for rows in FULL_ROWS)
         places = range(base % HALF, base % HALF + WRITE)
         spots = [slice(place * LANES, (place + 1) * LANES) for place in places]
         targets = [slice(pair * LANES, (pair + 1) * LANES) for pair in range(base, base + WRITE)]
@@ -329,20 +321,20 @@
             du[:, to] = got[half](slice(DECAY + place, DECAY + place + 1))
             loaded.append([by_head(part, heads) for part in halves(state) + halves(dstate)])
             across.append(full[FULL_TOK : FULL_TOK + 1, at] * jnp.sum(state * dstate, axis=0, keepdims=True))
-        reaches, pulls, values = [], [], []
+        reaches, pulls, values, paired = [], [], [], []
         for at, (sh, sl, dh, dlow) in zip(spots, loaded):
             gb, vb = g[:, at], v[:, at]
-            reaches.append(dot(cat(gb, gb, axis=1), cat(sh, sl, axis=0), NN))
-            pulls.append(dot(cat(vb, vb, axis=1), cat(dh, dlow, axis=0), NN))
-            eh, el = pk[:, at].astype(BF16), el_in[:, at]
+            reaches.append(rd[:, at] * dot(cat(gb, gb, axis=1), cat(sh, sl, axis=0), NN))
+            pulls.append(kd[:, at] * dot(cat(vb, vb, axis=1), cat(dh, dlow, axis=0), NN))
+            eh, el = halves(k[:, at].astype(F32) * kd[:, at])
             values.append(dot(cat(eh, el, axis=1), cat(dh, dh, axis=1), NT) + dot(eh, dlow, NT))
-        paired = []
         for at, reach, pull in zip(spots, reaches, pulls):
-            paired.append(cat(*halves(cat(pr[:, at] * reach, pk[:, at] * pull, axis=0)), axis=1))
+            rp, kp = r[:, at].astype(F32), k[:, at].astype(F32)
+            paired.append(cat(*halves(cat(rp * reach, kp * pull, axis=0)), axis=1))
         moved = [dot(sums, part, NN) for part in paired]
         for n, (at, to) in enumerate(zip(spots, targets)):
-            rounded[0, :, to] = (dri[:, at] + rd[:, at] * reaches[n]).astype(BF16)
-            rounded[1, :, to] = (dki[:, at] + kd[:, at] * pulls[n]).astype(BF16)
+            rounded[0, :, to] = (dri[:, at] + reaches[n]).astype(BF16)
+            rounded[1, :, to] = (dki[:, at] + pulls[n]).astype(BF16)
             rounded[2, :, to] = (dvi[:, at] + values[n]).astype(BF16)
             grad = dli[:, at] + moved[n][:, :LANES] + moved[n][:, LANES:] + across[n]
             rounded[3, :, to] = (rate[:, at] * grad).astype(BF16)
@@ -395,12 +387,12 @@
             in_specs=[whole] + [wide] * 5 + [pl.BlockSpec((1, part), lambda i: (0, i + here)), token],
             out_specs=[
                 pl.BlockSpec((FULL_TOK + 8, part), lambda i: (0, i)),
-                pl.BlockSpec((3 * TOK, part), lambda i: (0, i)),
+                pl.BlockSpec((4 * TOK, part), lambda i: (0, i)),
                 pl.BlockSpec((8, LANES), lambda i: (0, 0)),
             ],
             out_shape=[
                 pltpu.HBM((FULL_TOK + 8, HALF * LANES), F32),
-                pltpu.HBM((3 * TOK, HALF * LANES), BF16),
+                (pltpu.VMEM if half else pltpu.HBM)((4 * TOK, HALF * LANES), BF16),
                 pltpu.HBM((8, LANES), F32),
             ],
             scratch_shapes=[pltpu.VMEM((TOK, part), F32), pltpu.VMEM((4, TOK, LANES), F32)],
@@ -437,7 +429,7 @@
         cost_estimate=cost(10**6, 2 * 10**6),
     )(mine, theirs)
     got = exchange(packets, chips, "chip")
-    first, narrow_first, done = inside(0, combined)
+    *first, done = inside(0, combined)
     states, scanned = pl.pallas_call(
         scan_kernel,
         in_specs=[whole, token],
@@ -448,7 +440,7 @@
         cost_estimate=cost(10**10, 3 * 10**7),
     )(vm(got), hbm(done))
     returned = exchange(states, chips, "chip")
-    second, narrow_second, done = inside(1, scanned)
+    *second, done = inside(1, scanned)
     own, other = pl.pallas_call(
         expand_kernel,
         in_specs=[whole, whole, whole, token],
@@ -471,7 +463,7 @@
         name="final",
         compiler_params=params,
         cost_estimate=cost(10**9, 10**7),
-    )(vm(first), vm(narrow_first), vm(second), vm(narrow_second), vm(own), vm(other))
+    )(*(vm(part) for part in (*first, *second, own, other)))
     return dr, dk, dv, dx, du.reshape(width)
 
 

time: 58.7 us -> 58.3 us (level)
  waiting for transfers between devices: 14 us -> 14.8 us
  Pallas kernels: 21.8 us -> 21.2 us
    all_to_all x2, waiting for transfers between devices: 10.9 us -> 11.7 us  [exchange(): return lax.all_to_all(packets, axis, 0, 0, tiled=True).reshape(rows.shape)]
    pallas_call x2, Pallas kernels: 12.9 us -> 12.1 us  [inside(): pl.pallas_call(inside_kernel, grid=(HALF // INSIDE,), in_specs=[whole] +...]
  transfers between devices with their start and end apart: 4 -> 4, of which waited for: 4 -> 4; matrix products, arithmetic and copies ran while one was open for 0% -> 0% of each run, Pallas kernels for 22% -> 21%
where the time goes in v5:
time: 58.3 us; the launch traced here: 57.8 us
  Pallas kernels  21.2 us (36%)
  starting transfers between devices  21.1 us (36%)
  waiting for transfers between devices  14.8 us (25%)
  between operations  0.67 us (1%)
    all_to_all x2, starting transfers between devices, exchange(): return lax.all_to_all(packets, axis, 0, 0, tiled=True).reshape(rows.shape)  16.3 us
    pallas_call x2, Pallas kernels, inside(): pl.pallas_call(inside_kernel, grid=(HALF // INSIDE,), in_specs=[whole] +...  12.1 us
    all_to_all x2, waiting for transfers between devices, exchange(): return lax.all_to_all(packets, axis, 0, 0, tiled=True).reshape(rows.shape)  11.7 us
    ppermute x2, starting transfers between devices, swap(): return lax.ppermute(rows, 'core', [(0, 1), (1, 0)])  4.77 us
    pallas_call x1, Pallas kernels, body(): pl.pallas_call(summary_kernel, grid=(width // part,), in_specs=[whole] +...  3.56 us
    pallas_call x1, Pallas kernels, body(): pl.pallas_call(final_kernel, in_specs=[whole] * 6, out_specs=[pl.BlockSpe...  3.49 us
    ppermute x2, waiting for transfers between devices, swap(): return lax.ppermute(rows, 'core', [(0, 1), (1, 0)])  3.09 us
  transfers between devices with their start and end apart: 4, of which 4 were waited for; matrix products, arithmetic and copies ran while one was open for 0% of the time, Pallas kernels for 21%

profile of v5, /device:TPU:1, one launch (start us, length us, event | category | flops | bytes accessed | tf_op | source)
XLA Modules:
  0.0 57.8 jit_solution(6805334999635446409)
XLA Ops:
  0.6 3.6 %summary.1 = (f32[1040,128]{1,0:T(8,128)S(1)}, f32[1040,128]{1,0:T(8,128)S(1)}) custom-call(s32[1,256]{1,0:T(1,128)} %bitcast.12, bf16[128,2048]{1,0:T(8,128)(2,1)} %r.5, bf16[128,2048]{1,0:T(8,128)(2,1)} %k.5, bf16[128,2048]{1,0:T(8,128)(2,1)} %v.5, bf16[128,2048]{1,0:T(8,128)(2,1)} %g.5, f32[128,2048]{1,0:T(8,128)} %x.5), custom_call_target="tpu_custom_call" | custom-call | flops 1000000000 | bytes 6000000 | tf_op jit(solution)/shard_map/summary/pallas_call | solution.py:406
  4.2 1.5 %collective-permute-start = (f32[1040,128]{1,0:T(8,128)S(1)}, f32[1040,128]{1,0:T(8,128)S(1)}, u32[]{:S(2)}, u32[]{:S(2)}) collective-permute-start(f32[1040,128]{1,0:T(8,128)S(1)} %get-tuple-element.25), channel_id=1, source_target_pairs={{0,1},{1,0},{2,3},{3,2},{4,5},{5,4},{6,7},{7,6},{8,9},{9,8},{10,11... | collective-permute-start | bytes 1597448 | tf_op jit(solution)/shard_map/ppermute | solution.py:358
  5.7 1.5 %collective-permute-done.theirs = f32[1040,128]{1,0:T(8,128)S(1)} collective-permute-done((f32[1040,128]{1,0:T(8,128)S(1)}, f32[1040,128]{1,0:T(8,128)S(1)}, u32[]{:S(2)}, u32[]{:S(2)}) %collective-permute-start) | collective-permute-done | bytes 532512 | tf_op jit(solution)/shard_map/ppermute | solution.py:358
  7.2 0.9 %combine.1 = (f32[1152,128]{1,0:T(8,128)}, f32[8,128]{1,0:T(8,128)}) custom-call(f32[1040,128]{1,0:T(8,128)S(1)} %get-tuple-element.24.mine, f32[1040,128]{1,0:T(8,128)S(1)} %collective-permute-done.theirs), custom_call_target="tpu_custom_call" | custom-call | flops 1000000 | bytes 2000000 | tf_op jit(solution)/shard_map/combine/pallas_call | solution.py:422
  8.1 11.2 %all-to-all-start = ((f32[64,18,1,128]{3,2,1,0:T(1,128)}), f32[64,18,1,128]{3,2,1,0:T(1,128)S(1)}, u32[]{:S(2)}, u32[]{:S(2)}) async-start(f32[64,18,1,128]{3,2,1,0:T(1,128)} %bitcast.2), calls=%async_computation | async-start | bytes 1179648 | tf_op jit(solution)/shard_map/all_to_all | solution.py:363
  19.4 6.1 %inside.2 = (f32[904,1024]{1,0:T(8,128)}, bf16[512,1024]{1,0:T(8,128)(2,1)}, f32[8,128]{1,0:T(8,128)}) custom-call(s32[1,256]{1,0:T(1,128)} %bitcast.13, bf16[128,2048]{1,0:T(8,128)(2,1)} %r.5, bf16[128,2048]{1,0:T(8,128)(2,1)} %k.5, bf16[128,2048]{1,0:T(8,128)(2,1)} %v.5, bf16[128,2048]{1,0:T(8,128)(2,1)} %g.5, f32[128,2048]{1,0:T(8,128)} %x.5, ...), custom_call_target="tpu_custom_call" | custom-call | flops 10000000000 | bytes 10000000 | tf_op jit(solution)/shard_map/inside/pallas_call | solution.py:384
  25.4 6.6 %all-to-all-done = f32[64,18,1,128]{3,2,1,0:T(1,128)S(1)} async-done(((f32[64,18,1,128]{3,2,1,0:T(1,128)}), f32[64,18,1,128]{3,2,1,0:T(1,128)S(1)}, u32[]{:S(2)}, u32[]{:S(2)}) %all-to-all-start) | async-done | bytes 589856 | tf_op jit(solution)/shard_map/all_to_all | solution.py:363
  32.0 1.0 %scan.1 = (f32[1088,128]{1,0:T(8,128)}, f32[8,128]{1,0:T(8,128)}) custom-call(f32[1152,128]{1,0:T(8,128)S(1)} %bitcast.7, f32[8,128]{1,0:T(8,128)} %get-tuple-element.30.before), custom_call_target="tpu_custom_call" | custom-call | flops 10000000000 | bytes 30000000 | tf_op jit(solution)/shard_map/scan/pallas_call | solution.py:433
  33.0 5.1 %all-to-all-start.1 = ((f32[64,17,1,128]{3,2,1,0:T(1,128)}), f32[64,17,1,128]{3,2,1,0:T(1,128)S(1)}, u32[]{:S(2)}, u32[]{:S(2)}) async-start(f32[64,17,1,128]{3,2,1,0:T(1,128)} %bitcast.4), calls=%async_computation.1 | async-start | bytes 1114112 | tf_op jit(solution)/shard_map/all_to_all | solution.py:363
  38.1 6.0 %inside.3 = (f32[904,1024]{1,0:T(8,128)}, bf16[512,1024]{1,0:T(8,128)(2,1)S(1)}, f32[8,128]{1,0:T(8,128)}) custom-call(s32[1,256]{1,0:T(1,128)} %bitcast.14, bf16[128,2048]{1,0:T(8,128)(2,1)} %r.5, bf16[128,2048]{1,0:T(8,128)(2,1)} %k.5, bf16[128,2048]{1,0:T(8,128)(2,1)} %v.5, bf16[128,2048]{1,0:T(8,128)(2,1)} %g.5, f32[128,2048]{1,0:T(8,128)} %x.5, ...), custom_call_target="tpu_custom_call" | custom-call | flops 10000000000 | bytes 10000000 | tf_op jit(solution)/shard_map/inside/pallas_call | solution.py:384
  44.1 5.2 %all-to-all-done.1 = f32[64,17,1,128]{3,2,1,0:T(1,128)S(1)} async-done(((f32[64,17,1,128]{3,2,1,0:T(1,128)}), f32[64,17,1,128]{3,2,1,0:T(1,128)S(1)}, u32[]{:S(2)}, u32[]{:S(2)}) %all-to-all-start.1) | async-done | bytes 557088 | tf_op jit(solution)/shard_map/all_to_all | solution.py:363
  49.3 0.0 copy-start
  49.3 0.0 copy-start.1
  49.3 0.0 copy-start.2
  49.3 0.1 expand.1
  49.4 3.3 %collective-permute-start.1 = (f32[1032,128]{1,0:T(8,128)S(1)}, f32[1032,128]{1,0:T(8,128)S(1)}, u32[]{:S(2)}, u32[]{:S(2)}) collective-permute-start(f32[1032,128]{1,0:T(8,128)S(1)} %get-tuple-element.37), channel_id=1, source_target_pairs={{0,1},{1,0},{2,3},{3,2},{4,5},{5,4},{6,7},{7,6},{8,9},{9,8},{10,11... | collective-permute-start | bytes 1585160 | tf_op jit(solution)/shard_map/ppermute | solution.py:358
  52.7 1.5 %collective-permute-done.1.theirs = f32[1032,128]{1,0:T(8,128)S(1)} collective-permute-done((f32[1032,128]{1,0:T(8,128)S(1)}, f32[1032,128]{1,0:T(8,128)S(1)}, u32[]{:S(2)}, u32[]{:S(2)}) %collective-permute-start.1) | collective-permute-done | bytes 528416 | tf_op jit(solution)/shard_map/ppermute | solution.py:358
  54.3 0.0 copy-done
  54.3 0.0 copy-done.1
  54.3 0.0 copy-done.2
  54.3 3.5 %final.1 = (bf16[128,2048]{1,0:T(8,128)(2,1)}, bf16[128,2048]{1,0:T(8,128)(2,1)}, bf16[128,2048]{1,0:T(8,128)(2,1)}, bf16[128,2048]{1,0:T(8,128)(2,1)}, f32[1,2048]{1,0:T(1,128)}) custom-call(f32[904,1024]{1,0:T(8,128)S(1)} %copy-done, bf16[512,1024]{1,0:T(8,128)(2,1)S(1)} %copy-done.2, f32[904,1024]{1,0:T(8,128)S(1)} %copy-done.1, ...), custom_call_target="tpu_custom_call" | custom-call | flops 1000000000 | bytes 10000000 | tf_op jit(solution)/shard_map/final/pallas_call | solution.py:454
Async XLA Ops:
  4.2 3.0 %collective-permute-start = (f32[1040,128]{1,0:T(8,128)S(1)}, f32[1040,128]{1,0:T(8,128)S(1)}, u32[]{:S(2)}, u32[]{:S(2)}) collective-permute-start(f32[1040,128]{1,0:T(8,128)S(1)} %get-tuple-element.25), channel_id=1, source_target_pairs={{0,1},{1,0},{2,3},{3,2},{4,5},{5,4},{6,7},{7,6},{8,9},{9,8},{10,11... | collective-permute-start | bytes 1597448 | tf_op jit(solution)/shard_map/ppermute | solution.py:358
  8.1 23.9 %all-to-all-start = ((f32[64,18,1,128]{3,2,1,0:T(1,128)}), f32[64,18,1,128]{3,2,1,0:T(1,128)S(1)}, u32[]{:S(2)}, u32[]{:S(2)}) async-start(f32[64,18,1,128]{3,2,1,0:T(1,128)} %bitcast.2), calls=%async_computation | async-start | bytes 1179648 | tf_op jit(solution)/shard_map/all_to_all | solution.py:363
  33.0 16.2 %all-to-all-start.1 = ((f32[64,17,1,128]{3,2,1,0:T(1,128)}), f32[64,17,1,128]{3,2,1,0:T(1,128)S(1)}, u32[]{:S(2)}, u32[]{:S(2)}) async-start(f32[64,17,1,128]{3,2,1,0:T(1,128)} %bitcast.4), calls=%async_computation.1 | async-start | bytes 1114112 | tf_op jit(solution)/shard_map/all_to_all | solution.py:363
  49.3 5.0 %copy-start = (f32[904,1024]{1,0:T(8,128)S(1)}, f32[904,1024]{1,0:T(8,128)}, u32[]{:S(2)}) copy-start(f32[904,1024]{1,0:T(8,128)} %get-tuple-element.27.full_a) | copy-start | bytes 11108356
  49.3 5.0 %copy-start.1 = (f32[904,1024]{1,0:T(8,128)S(1)}, f32[904,1024]{1,0:T(8,128)}, u32[]{:S(2)}) copy-start(f32[904,1024]{1,0:T(8,128)} %get-tuple-element.32.full_b) | copy-start | bytes 11108356
  49.3 5.0 %copy-start.2 = (bf16[512,1024]{1,0:T(8,128)(2,1)S(1)}, bf16[512,1024]{1,0:T(8,128)(2,1)}, u32[]{:S(2)}) copy-start(bf16[512,1024]{1,0:T(8,128)(2,1)} %get-tuple-element.28.kept_a) | copy-start | bytes 3145732
  49.4 4.9 %collective-permute-start.1 = (f32[1032,128]{1,0:T(8,128)S(1)}, f32[1032,128]{1,0:T(8,128)S(1)}, u32[]{:S(2)}, u32[]{:S(2)}) collective-permute-start(f32[1032,128]{1,0:T(8,128)S(1)} %get-tuple-element.37), channel_id=1, source_target_pairs={{0,1},{1,0},{2,3},{3,2},{4,5},{5,4},{6,7},{7,6},{8,9},{9,8},{10,11... | collective-permute-start | bytes 1585160 | tf_op jit(solution)/shard_map/ppermute | solution.py:358
